TPU v7x, 128 devices: a whole 4x4x4 slice. The times are simulated.
128 devices in a mesh: wide: 32 (over x, z, core), narrow: 4 (over y).
Axes of the slice: x: 4, y: 4, z: 4, core: 2. Of those that a mesh axis runs over, the one named last changes fastest.
Arguments:
- tokens: bfloat16 [262144, 1024], P(('wide', 'narrow')), may hold values from -64 to 64
- slot_params: bfloat16 [1024, 512], replicated, may hold values from -2.5 to 2.5
- expert_in: bfloat16 [128, 1024, 4096], P('wide', None, 'narrow'), may hold values from -0.1875 to 0.1875
- expert_out: bfloat16 [128, 4096, 1024], P('wide', 'narrow'), may hold values from -0.09375 to 0.09375
Outputs:
- mixed: bfloat16 [262144, 1024], P(('wide', 'narrow'))
All inputs are finite; a program needn't handle non-finite values.
Results may differ from a plain program's by a relative error of at most 0.0071.
Values may be sent and summed in bfloat16 or wider, within the bound.
A program may use at most 128 MiB of HBM per device.

v0:
```python
import jax
import jax.numpy as jnp
from jax import lax
from jax.sharding import PartitionSpec as P

SLOT_PER = 4


def divide_rows(summed, slot_totals):
    return (summed / slot_totals[:, None]).astype(jnp.bfloat16)


def shards(tokens, slot_params, expert_in, expert_out):
    logits = jnp.dot(tokens, slot_params, preferred_element_type=jnp.float32)
    local_peak = jnp.max(logits, axis=0)
    column_peak = lax.pmax(local_peak, ("wide", "narrow"))
    weights = jnp.exp(logits - column_peak)
    slot_totals = lax.psum(jnp.sum(weights, axis=0), ("wide", "narrow"))
    dispatch = weights.astype(jnp.bfloat16)
    slot_count = slot_params.shape[1]
    row_count = slot_count // lax.axis_size("wide")
    columns = dispatch
    partial_value = lax.psum_scatter(
        lax.dot_general(
            columns, tokens, (((0,), (0,)), ((), ())), preferred_element_type=jnp.float32
        ),
        "wide",
        scatter_dimension=0,
        tiled=True,
    )
    summed = lax.psum(partial_value, "narrow")
    owned_totals = lax.dynamic_slice_in_dim(
        slot_totals, lax.axis_index("wide") * row_count, row_count
    )
    slot_in = divide_rows(summed, owned_totals)
    slot_stack = slot_in.reshape(expert_in.shape[0], SLOT_PER, slot_in.shape[1])
    hidden = jax.nn.gelu(
        jnp.einsum("esd,edh->esh", slot_stack, expert_in, preferred_element_type=jnp.float32)
    ).astype(jnp.bfloat16)
    expert_sum = jnp.einsum("esh,ehd->esd", hidden, expert_out, preferred_element_type=jnp.float32)
    expert_sum = expert_sum.reshape(-1, expert_sum.shape[2])
    mixing = jax.nn.softmax(logits, axis=1).astype(jnp.bfloat16)
    whole_rows = lax.psum(expert_sum, "narrow").astype(jnp.bfloat16)
    columns = mixing
    mixed = jnp.dot(
        columns,
        lax.all_gather(whole_rows, "wide", axis=0, tiled=True),
        preferred_element_type=jnp.float32,
    )
    return mixed.astype(jnp.bfloat16)


def solution(mesh):
    return jax.shard_map(
        shards,
        mesh=mesh,
        in_specs=(
            P(("wide", "narrow"), None),
            P(),
            P("wide", None, "narrow"),
            P("wide", "narrow", None),
        ),
        out_specs=P(("wide", "narrow"), None),
        check_vma=False,
    )
```

profile of v0, /device:TPU:1, one launch (start us, length us, event | category | flops | bytes accessed | tf_op | source)
XLA Modules:
  0.0 312.3 jit_solution(13459068889585292751)
XLA Ops:
  6.5 0.0 copy-start
  6.5 0.0 reduce-scatter.2.cloned.1.call-start
  6.5 1.2 copy-done
  7.8 6.5 %fusion.26 = (f32[2048]{0:T(1024)S(1)}, f32[512]{0:T(512)S(1)}, f32[2048,512]{1,0:T(8,128)}) fusion(bf16[2048,1024]{1,0:T(8,128)(2,1)} %param.4, bf16[1024,512]{1,0:T(8,128)(2,1)S(1)} %copy-done), kind=kOutput, calls=%fused_computation.30 | convolution fusion | flops 2149578240 | bytes 9447424 | tf_op jit(solution)/shard_map/dot_general | solution.py:14
  14.2 68.6 %pmax.7 = f32[512]{0:T(512)S(1)} all-reduce(f32[512]{0:T(512)S(1)} %get-tuple-element.8), channel_id=1, replica_groups=mesh['wide'=32,'narrow'=4] {'wide','narrow'}, use_global_device_ids=true, to_apply=%region_3.0 | all-reduce | flops 512 | bytes 4096 | tf_op jit(solution)/shard_map/pmax | solution.py:16
  82.8 7.2 %fusion.3 = f32[512,1024]{1,0:T(8,128)} fusion(bf16[2048,1024]{1,0:T(8,128)(2,1)} %param.4, f32[2048,512]{1,0:T(8,128)} %get-tuple-element.9, f32[512]{0:T(512)S(1)} %pmax.7), kind=kOutput, calls=%fused_computation.7 | convolution fusion | flops 2149580800 | bytes 10487808 | tf_op jit(solution)/shard_map/dot_general | solution.py:24
  90.0 0.0 reduce-scatter.2.cloned.1.call-update
  90.0 0.0 all-reduce.2.cloned.1.call-start
  90.1 73.9 %reduce-scatter.2.cloned.1.call-done = f32[16,1024]{1,0:T(8,128)} async-done(((f32[512,1024]{1,0:T(8,128)}), f32[16,1024]{1,0:T(8,128)}) %reduce-scatter.2.cloned.1.call-update) | async-done | bytes 65552 | tf_op jit(solution)/shard_map/reduce_scatter | solution.py:23
  163.9 0.0 all-reduce.2.cloned.1.call-update
  164.0 0.0 all-gather.2.cloned.1.call-start
  164.0 3.1 %fusion = (f32[2048]{0:T(1024)S(1)}, f32[512]{0:T(512)S(1)}) fusion(f32[2048,512]{1,0:T(8,128)} %get-tuple-element.9, f32[2048]{0:T(1024)S(1)} %get-tuple-element.7, f32[512]{0:T(512)S(1)} %pmax.7), kind=kLoop, calls=%fused_computation.4 | loop fusion | flops 4191744 | bytes 4214784 | tf_op jit(solution)/shard_map/reduce_sum | solution.py:42
  167.2 66.0 %psum.22 = f32[512]{0:T(512)S(1)} all-reduce(f32[512]{0:T(512)S(1)} %get-tuple-element.6), channel_id=1, replica_groups=mesh['wide'=32,'narrow'=4] {'wide','narrow'}, use_global_device_ids=true, to_apply=%region_7.0 | all-reduce | flops 512 | bytes 4096 | tf_op jit(solution)/shard_map/psum | solution.py:18
  233.2 0.1 dynamic_slice.3
  233.3 0.0 all-reduce.2.cloned.1.call-done
  233.3 0.9 divide_convert_fusion.2
  234.2 8.0 %fusion.16 = f32[4,4,1024]{2,1,0:T(4,128)S(1)} fusion(bf16[4,1024,1024]{2,1,0:T(8,128)(2,1)} %param.7, bf16[4,4,1024]{2,1,0:T(4,128)(2,1)S(1)} %reshape.10, bf16[4,1024,1024]{2,1,0:T(8,128)(2,1)} %param.6), kind=kOutput, calls=%fused_computation.21 | convolution fusion | flops 67256320 | bytes 16875520 | tf_op jit(solution)/shard_map/esh,ehd->esd/dot_general | solution.py:40
  242.3 12.6 %psum.23 = bf16[16,1024]{1,0:T(8,128)(2,1)} all-reduce(f32[16,1024]{1,0:T(8,128)S(1)} %reshape.11), channel_id=1, replica_groups=mesh['wide'=32,'narrow'=4] {'narrow'}, use_global_device_ids=true, to_apply=%region_8.0 | all-reduce | flops 16384 | bytes 98304 | tf_op jit(solution)/shard_map/psum | solution.py:43
  254.9 0.0 all-gather.2.cloned.1.call-update
  254.9 43.9 %all-gather.2.cloned.1.call-done = bf16[512,1024]{1,0:T(8,128)(2,1)} async-done(((bf16[16,1024]{1,0:T(8,128)(2,1)}), bf16[512,1024]{1,0:T(8,128)(2,1)}) %all-gather.2.cloned.1.call-update) | async-done | bytes 1048592 | tf_op jit(solution)/shard_map/all_gather | solution.py:47
  298.7 7.0 %convolution_convert_fusion = bf16[2048,1024]{1,0:T(8,128)(2,1)} fusion(bf16[512,1024]{1,0:T(8,128)(2,1)} %all-gather.2.cloned.1.call-done, f32[2048,512]{1,0:T(8,128)} %get-tuple-element.9, f32[2048]{0:T(1024)S(1)} %get-tuple-element.5, f32[2048]{0:T(1024)S(1)} %get-tuple-element.7), kind=kOutput, calls=%fused_computation.3 | convolution fusion | flops 2152726528 | bytes 9453568 | tf_op jit(solution)/shard_map/dot_general | solution.py:45
  (2 shorter events, 0.1 us)
Async XLA Ops:
  6.5 1.2 copy-start
  6.5 157.4 %reduce-scatter.2.cloned.1.call-start = ((), (), s32[]{:S(2)}) async-start(), calls=%async_computation.1 | async-start | bytes 2162688 | tf_op jit(solution)/shard_map/reduce_scatter | solution.py:23
  90.0 143.2 %all-reduce.2.cloned.1.call-start = ((), (), s32[]{:S(2)}) async-start(), calls=%async_computation.2 | async-start | bytes 131072 | tf_op jit(solution)/shard_map/psum | solution.py:31
  164.0 134.8 %all-gather.2.cloned.1.call-start = ((), (), s32[]{:S(2)}) async-start(), calls=%async_computation.3 | async-start | bytes 1081344 | tf_op jit(solution)/shard_map/all_gather | solution.py:47
Sparse Core Ops, SparseCore 0:
  90.2 73.7 reduce-scatter.1
  166.2 40.1 all-reduce.1
  255.0 43.6 all-gather.1
where the time goes:
time: 313 us; the launch traced here: 312 us
  blocking collectives  147 us (47%)
  waiting for transfers between devices  118 us (38%)
  matrix products  28.7 us (9%)
  between operations  13.1 us (4%)
  other arithmetic  4.06 us (1%)
    reduce_scatter x1, waiting for transfers between devices, shards(): lax.psum_scatter(lax.dot_general(columns, tokens, (((0,), (0,)), ((), ())...  73.9 us
    pmax x1, blocking collectives, shards(): column_peak = lax.pmax(local_peak, ('wide', 'narrow'))  68.6 us
    psum x1, blocking collectives, shards(): slot_totals = lax.psum(jnp.sum(weights, axis=0), ('wide', 'narrow'))  66 us
    all_gather x1, waiting for transfers between devices, shards(): lax.all_gather(whole_rows, 'wide', axis=0, tiled=True)  43.9 us
    psum x1, blocking collectives, shards(): whole_rows = lax.psum(expert_sum, 'narrow').astype(jnp.bfloat16)  12.6 us
    dot_general x1, matrix products, shards(): jnp.einsum('esh,ehd->esd', hidden, expert_out, preferred_element_type=jnp...  8.04 us
    dot_general x1, matrix products, shards(): lax.dot_general(columns, tokens, (((0,), (0,)), ((), ())), preferred_elem...  7.15 us
    dot_general x1, matrix products, shards(): jnp.dot(columns, lax.all_gather(whole_rows, 'wide', axis=0, tiled=True),...  7.05 us
  transfers between devices with their start and end apart: 3, of which 2 were waited for; matrix products, arithmetic and copies ran while one was open for 1% of the time, Pallas kernels for 0%

commit v1 on v0

v1 whole, which is shorter than its diff:
```python
import jax
import jax.numpy as jnp
from jax import lax
from jax.experimental import pallas as pl
from jax.experimental.pallas import tpu as pltpu
from jax.sharding import PartitionSpec as P

MESH = pl.DeviceIdType.MESH
F32, BF16 = jnp.float32, jnp.bfloat16
NX, NZ, NY, NC = 4, 4, 4, 2
XZ = NX * NZ
CHIPS = XZ * NY
ROWS = 16
TOK, D, S, H = 2048, 1024, 512, 1024
COLS = D // NY
TCH = 512
NT = TOK // TCH


def dot(a, b):
    return jnp.dot(a, b, preferred_element_type=F32)


def layer_kernel(
    tok_hbm, par_hbm, win_hbm, wout_hbm, out_hbm,
    tok, par, win, wout, logits, disp_t, comb, sums, part, outb, recv,
    peak_own, peak_other, tot_own, tot_other, stats, stats_recv,
    sin, obuf, orecv, so, stage,
    in_sem, w_sem, peak_s, peak_r, tot_s, tot_r, part_s, part_r,
    sc_s, sc_r, st_s, st_r, sin_s, sin_r, o_s, o_r, ag_s, ag_r, fw_s, fw_r, out_sem,
):
    wide = lax.axis_index("wide")
    y = lax.axis_index("narrow")
    core = wide % NC
    xz = wide // NC
    x, z = xz // NZ, xz % NZ
    me = xz * NY + y

    def where_is(k):
        dx, dz = k // NZ, k % NZ
        return ((x + dx) % NX) * NZ + (z + dz) % NZ

    def device(to_xz, to_y):
        return {"wide": to_xz * NC + core, "narrow": to_y}

    other = {"wide": xz * NC + 1 - core, "narrow": y}

    def tok_copy(i):
        rows = pl.ds(i * TCH, TCH)
        return pltpu.make_async_copy(tok_hbm.at[rows], tok.at[rows], in_sem.at[i])

    par_copy = pltpu.make_async_copy(par_hbm, par, in_sem.at[NT])
    par_copy.start()
    for i in range(NT):
        tok_copy(i).start()

    barrier = pltpu.get_barrier_semaphore()

    def greet(k, carry):
        to_xz, to_y = where_is(k // NY), (y + k % NY) % NY
        pl.semaphore_signal(barrier, inc=1, device_id=device(to_xz, to_y), device_id_type=MESH)
        return carry

    pl.semaphore_signal(barrier, inc=1, device_id=other, device_id_type=MESH)
    lax.fori_loop(1, CHIPS, greet, 0)

    par_copy.wait()

    def logits_step(i, peak):
        tok_copy(i).wait()
        rows = pl.ds(pl.multiple_of(i * TCH, TCH), TCH)
        block = dot(tok[rows, :], par[...])
        logits[rows, :] = block
        return jnp.maximum(peak, jnp.max(block, axis=0, keepdims=True))

    peak = lax.fori_loop(0, NT, logits_step, jnp.full((1, S), -jnp.inf, F32))

    win_copy = pltpu.make_async_copy(win_hbm, win, w_sem.at[0])
    wout_copy = pltpu.make_async_copy(wout_hbm, wout, w_sem.at[1])
    win_copy.start()
    wout_copy.start()

    def remote(src, dst, send, recv_sem, to):
        return pltpu.make_async_remote_copy(
            src_ref=src, dst_ref=dst, send_sem=send, recv_sem=recv_sem,
            device_id=to, device_id_type=MESH,
        )

    peak_own[...] = jnp.broadcast_to(peak, (8, S))
    pl.semaphore_wait(barrier, CHIPS)
    peak_copy = remote(peak_own, peak_other, peak_s, peak_r, other)
    peak_copy.start()

    def soften(i, carry):
        rows = pl.ds(pl.multiple_of(i * 256, 256), 256)
        block = logits[rows, :]
        e = jnp.exp(block - jnp.max(block, axis=1, keepdims=True))
        comb[rows, :] = (e / jnp.sum(e, axis=1, keepdims=True)).astype(BF16)
        return carry

    lax.fori_loop(0, 3, soften, 0)
    peak_copy.wait()
    peak = jnp.maximum(peak, peak_other[0:1, :])

    def weigh(i, total):
        rows = pl.ds(pl.multiple_of(i * 256, 256), 256)
        w = jnp.exp(logits[rows, :] - peak)
        disp_t[:, rows] = jnp.transpose(w).astype(BF16)
        return total + jnp.sum(w, axis=0, keepdims=True)

    total = lax.fori_loop(0, TOK // 256, weigh, jnp.zeros((1, S), F32))
    tot_own[...] = jnp.broadcast_to(total, (8, S))
    tot_copy = remote(tot_own, tot_other, tot_s, tot_r, other)
    tot_copy.start()

    def part_copy(j):
        return remote(sums.at[j, :, 1 - core], part.at[j], part_s.at[j], part_r.at[j], other)

    def matmul_step(j):
        to_y = (y + j) % NY
        cols = pl.ds(pl.multiple_of(to_y * COLS, COLS), COLS)
        block = dot(disp_t[...], tok[:, cols])
        sums[j] = block.astype(BF16).reshape(XZ, NC, ROWS, COLS)
        part_copy(j).start()

    def send_step(j):
        to_y = (y + j) % NY
        part_copy(j).wait()
        outb[j] = (sums[j, :, core].astype(F32) + part[j].astype(F32)).astype(BF16)

        def send(k, carry):
            to_xz = where_is(k)
            remote(outb.at[j, to_xz], recv.at[me], sc_s, sc_r, device(to_xz, to_y)).start()
            remote(
                stats.at[to_xz * NC + core], stats_recv.at[me], st_s, st_r, device(to_xz, to_y)
            ).start()
            return carry

        @pl.when(j == 0)
        def _():
            recv[me] = outb[0, xz]
            stats_recv[me] = stats[xz * NC + core]

        lax.fori_loop(jnp.where(j == 0, 1, 0), XZ, send, 0)

    matmul_step(0)
    tot_copy.wait()
    total = total + tot_other[0:1, :]
    lane = lax.broadcasted_iota(jnp.int32, (S // ROWS, ROWS, 128), 2)
    row = lax.broadcasted_iota(jnp.int32, (S // ROWS, ROWS, 128), 1)
    peak_rows = jnp.transpose(jnp.broadcast_to(peak, (128, S))).reshape(S // ROWS, ROWS, 128)
    tot_rows = jnp.transpose(jnp.broadcast_to(total, (128, S))).reshape(S // ROWS, ROWS, 128)
    packed = jnp.where(lane == row, peak_rows, 0.0) + jnp.where(lane == row + ROWS, tot_rows, 0.0)
    stats[...] = jnp.sum(packed, axis=1, keepdims=True)

    def pipe(j, carry):
        matmul_step(j)
        send_step(j - 1)
        return carry

    lax.fori_loop(1, NY, pipe, 0)
    send_step(NY - 1)

    lax.fori_loop(3, TOK // 256, soften, 0)

    def drain(ref, sem):
        pltpu.make_async_copy(ref, ref, sem).wait()

    drain(stats_recv.at[pl.ds(0, CHIPS - 1)], st_r)
    drain(recv.at[pl.ds(0, CHIPS - 1)], sc_r)

    got = stats_recv[...].reshape(CHIPS, 128)
    top = jnp.max(got, axis=0, keepdims=True)
    factor = jnp.exp(jnp.minimum(got - top, 0.0))
    scaled = factor * pltpu.roll(got, 128 - ROWS, 1)
    turned = jnp.transpose(jnp.concatenate([factor, scaled], axis=0))[0:ROWS, :]
    owned = jnp.sum(turned[:, CHIPS:], axis=1, keepdims=True)
    acc = jnp.zeros((ROWS, COLS), F32)
    for q in range(CHIPS):
        acc = acc + turned[:, q : q + 1] * recv[q].astype(F32)
    sin[y] = (acc / owned).astype(BF16)

    def sin_copy(k):
        return remote(
            sin.at[y], sin.at[y], sin_s.at[k - 1], sin_r.at[k - 1],
            {"wide": wide, "narrow": (y + k) % NY},
        )

    for k in range(1, NY):
        sin_copy(k).start()
    win_copy.wait()
    wout_copy.wait()
    for k in range(1, NY):
        sin_copy(k).wait()

    expert = lax.broadcasted_iota(jnp.int32, (ROWS, H), 0) // 4
    slot_in = jnp.concatenate([sin[n] for n in range(NY)], axis=1)
    hidden = jnp.zeros((ROWS, H), F32)
    for e in range(4):
        hidden = jnp.where(expert == e, dot(slot_in, win[e]), hidden)
    hidden = jax.nn.gelu(hidden).astype(BF16).astype(F32)
    total_out = jnp.zeros((ROWS, D), F32)
    for e in range(4):
        total_out = total_out + dot(jnp.where(expert == e, hidden, 0.0).astype(BF16), wout[e])
    for n in range(NY):
        obuf[n] = total_out[:, n * COLS : (n + 1) * COLS]

    def o_copy(k):
        to_y = (y + k) % NY
        return remote(
            obuf.at[to_y], orecv.at[y], o_s.at[k - 1], o_r.at[k - 1], {"wide": wide, "narrow": to_y}
        )

    for k in range(1, NY):
        o_copy(k).start()
    orecv[y] = obuf[y]
    for k in range(1, NY):
        o_copy(k).wait()
    mine = orecv[0] + orecv[1] + orecv[2] + orecv[3]
    cols = pl.ds(pl.multiple_of(y * COLS, COLS), COLS)
    so[xz, core, :, cols] = mine.astype(BF16)

    def spread(k, carry):
        to_xz, to_y = where_is(k // NY), (y + k % NY) % NY
        block = so.at[xz, core, :, cols]
        remote(block, block, ag_s, ag_r.at[k // (CHIPS // NX)], device(to_xz, to_y)).start()
        return carry


    lax.fori_loop(1, CHIPS, spread, 0)

    def forward(dx):
        fx = (x - dx + NX) % NX
        block = so.at[pl.ds(fx * NZ, NZ), core]
        return remote(block, block, fw_s.at[dx], fw_r.at[dx], other)

    for dx in range(NX):
        n = (CHIPS // NX) - (1 if dx == 0 else 0)
        drain(recv.at[pl.ds(0, n)], ag_r.at[dx])
        forward(dx).start()
    for dx in range(NX):
        forward(dx).wait()

    def out_copy(i):
        rows = pl.ds(pl.multiple_of(i * TCH, TCH), TCH)
        return pltpu.make_async_copy(stage.at[rows], out_hbm.at[rows], out_sem.at[i])

    def mix(i, carry):
        rows = pl.ds(pl.multiple_of(i * TCH, TCH), TCH)
        stage[rows, :] = dot(comb[rows, :], so[...].reshape(S, D)).astype(BF16)
        out_copy(i).start()
        return carry

    lax.fori_loop(0, NT, mix, 0)
    drain(stats_recv.at[pl.ds(0, CHIPS - 1)], st_s)
    drain(recv.at[pl.ds(0, CHIPS - 1)], sc_s)
    drain(recv.at[pl.ds(0, CHIPS - 1)], ag_s)
    for i in range(NT):
        out_copy(i).wait()


def shards(tokens, slot_params, expert_in, expert_out):
    dma, vmem = pltpu.SemaphoreType.DMA, pltpu.VMEM
    return pl.pallas_call(
        layer_kernel,
        out_shape=jax.ShapeDtypeStruct((TOK, D), BF16),
        in_specs=[pl.BlockSpec(memory_space=pl.ANY)] * 4,
        out_specs=pl.BlockSpec(memory_space=pl.ANY),
        scratch_shapes=[
            vmem((TOK, D), BF16),
            vmem((D, S), BF16),
            vmem((4, D, H), BF16),
            vmem((4, H, D), BF16),
            vmem((TOK, S), F32),
            vmem((S, TOK), BF16),
            vmem((TOK, S), BF16),
            vmem((NY, XZ, NC, ROWS, COLS), BF16),
            vmem((NY, XZ, ROWS, COLS), BF16),
            vmem((NY, XZ, ROWS, COLS), BF16),
            vmem((CHIPS, ROWS, COLS), BF16),
            vmem((8, S), F32),
            vmem((8, S), F32),
            vmem((8, S), F32),
            vmem((8, S), F32),
            vmem((S // ROWS, 1, 128), F32),
            vmem((CHIPS, 1, 128), F32),
            vmem((NY, ROWS, COLS), BF16),
            vmem((NY, ROWS, COLS), F32),
            vmem((NY, ROWS, COLS), F32),
            vmem((XZ, NC, ROWS, D), BF16),
            vmem((TOK, D), BF16),
            dma((NT + 1,)),
            dma((2,)),
            dma, dma, dma, dma,
            dma((NY,)), dma((NY,)),
            dma, dma, dma, dma,
            dma((NY - 1,)), dma((NY - 1,)),
            dma((NY - 1,)), dma((NY - 1,)),
            dma, dma((NX,)),
            dma((NX,)), dma((NX,)),
            dma((NT,)),
        ],
        compiler_params=pltpu.CompilerParams(
            collective_id=0, has_side_effects=True, vmem_limit_bytes=60 * 1024 * 1024
        ),
        name="layer",
    )(tokens, slot_params, expert_in, expert_out)


def solution(mesh):
    return jax.shard_map(
        shards,
        mesh=mesh,
        in_specs=(
            P(("wide", "narrow"), None),
            P(),
            P("wide", None, "narrow"),
            P("wide", "narrow", None),
        ),
        out_specs=P(("wide", "narrow"), None),
        check_vma=False,
    )
```

time: 313 us -> 56.8 us (0.18)
  blocking collectives: 147 us -> 0 us
  waiting for transfers between devices: 118 us -> 0 us
  Pallas kernels: 0 us -> 52 us
  matrix products: 28.7 us -> 0 us
  between operations: 13.1 us -> 0.01 us
  other arithmetic: 4.06 us -> 0 us
  local copies, waits for them, and re-layouts: 1.35 us -> 4.64 us
    psum x2 -> x0, blocking collectives: 78.6 us -> none  [the longest x1 66 us: shards(): slot_totals = lax.psum(jnp.sum(weights, axis=0), ('wide', 'narrow'))]
    reduce_scatter x1 -> x0, waiting for transfers between devices: 73.9 us -> none  [shards(): lax.psum_scatter(lax.dot_general(columns, tokens, (((0,), (0,)), ((), ())...]
    pmax x1 -> x0, blocking collectives: 68.6 us -> none  [shards(): column_peak = lax.pmax(local_peak, ('wide', 'narrow'))]
    pallas_call x0 -> x1, Pallas kernels: none -> 52 us  [shards(): pl.pallas_call(layer_kernel, out_shape=jax.ShapeDtypeStruct((TOK, D), BF1...]
    all_gather x1 -> x0, waiting for transfers between devices: 43.9 us -> none  [shards(): lax.all_gather(whole_rows, 'wide', axis=0, tiled=True)]
    dot_general x4 -> x0, matrix products: 28.7 us -> none  [the longest x1 8.04 us: shards(): jnp.einsum('esh,ehd->esd', hidden, expert_out, preferred_element_type=jnp...]
    unnamed x2 -> x1, local copies, waits for them, and re-layouts: 1.22 us -> 4.64 us
    reduce_sum x1 -> x0, other arithmetic: 3.15 us -> none  [shards(): mixing = jax.nn.softmax(logits, axis=1).astype(jnp.bfloat16)]
  transfers between devices with their start and end apart: 3 -> 0, of which waited for: 2 -> 0; matrix products, arithmetic and copies ran while one was open for 1% -> 0% of each run, Pallas kernels for 0% -> 0%
where the time goes in v1:
time: 56.8 us; the launch traced here: 56.7 us
  Pallas kernels  52 us (92%)
  local copies, waits for them, and re-layouts  4.64 us (8%)
    pallas_call x1, Pallas kernels, shards(): pl.pallas_call(layer_kernel, out_shape=jax.ShapeDtypeStruct((TOK, D), BF1...  52 us
    unnamed x1, local copies, waits for them, and re-layouts  4.64 us

profile of v1, /device:TPU:1, one launch (start us, length us, event | category | flops | bytes accessed | tf_op | source)
XLA Modules:
  0.0 56.7 jit_solution(3512308834520187644)
XLA Ops:
  0.0 52.0 %layer.1 = bf16[2048,1024]{1,0:T(8,128)(2,1)} custom-call(bf16[2048,1024]{1,0:T(8,128)(2,1)} %tok_hbm.1, bf16[1024,512]{1,0:T(8,128)(2,1)} %par_hbm.1, bf16[4,1024,1024]{2,1,0:T(8,128)(2,1)} %win_hbm.1, bf16[4,1024,1024]{2,1,0:T(8,128)(2,1)} %wout_hbm.1), custom_call_target="tpu_custom_call" | custom-call | tf_op jit(solution)/shard_map/layer/pallas_call | solution.py:264
  52.0 4.6 %copy.6 = bf16[2048,1024]{1,0:T(8,128)(2,1)} copy(bf16[2048,1024]{1,0:T(8,128)(2,1)} %layer.1) | data formatting | bytes 8388608

commit v2 on v0

v2 whole, which is shorter than its diff:
```python
import jax
import jax.numpy as jnp
from jax import lax
from jax.experimental import pallas as pl
from jax.experimental.pallas import tpu as pltpu
from jax.sharding import PartitionSpec as P

MESH = pl.DeviceIdType.MESH
F32, BF16 = jnp.float32, jnp.bfloat16
NX, NZ, NY, NC = 4, 4, 4, 2
XZ = NX * NZ
ROWS = 16
TOK, D, S, H = 2048, 1024, 512, 1024
TCH = 512
NT = TOK // TCH
HALF = D // 2


def dot(a, b):
    return jnp.dot(a, b, preferred_element_type=F32)


def layer_kernel(
    tok_hbm, par_hbm, win_hbm, wout_hbm, out,
    tok, par, win, wout, logits, disp_t, comb, own, give, part, outb, recv,
    core_own, core_other, stats, stats_recv, ybuf, ystat, obuf, so,
    in_sem, w_sem, core_s, core_r, part_s, part_r,
    sc_s, sc_r, st_s, st_r, y_s, y_r, yst_s, yst_r, o_s, o_r, ag_s, ag_r, fw_s, fw_r,
):
    wide = lax.axis_index("wide")
    y = lax.axis_index("narrow")
    core = wide % NC
    xz = wide // NC
    x, z = xz // NZ, xz % NZ

    def where_is(k):
        dx, dz = k // NZ, k % NZ
        return ((x + dx) % NX) * NZ + (z + dz) % NZ

    def device(to_xz):
        return {"wide": to_xz * NC + core, "narrow": y}

    def along_y(k):
        return {"wide": wide, "narrow": (y + k) % NY}

    other = {"wide": xz * NC + 1 - core, "narrow": y}

    def remote(src, dst, send, recv_sem, to):
        return pltpu.make_async_remote_copy(
            src_ref=src, dst_ref=dst, send_sem=send, recv_sem=recv_sem,
            device_id=to, device_id_type=MESH,
        )

    def drain(ref, sem):
        pltpu.make_async_copy(ref, ref, sem).wait()

    def tok_copy(i):
        rows = pl.ds(i * TCH, TCH)
        return pltpu.make_async_copy(tok_hbm.at[rows], tok.at[rows], in_sem.at[i])

    par_copy = pltpu.make_async_copy(par_hbm, par, in_sem.at[NT])
    par_copy.start()
    for i in range(NT):
        tok_copy(i).start()

    barrier = pltpu.get_barrier_semaphore()

    def greet(to):
        pl.semaphore_signal(barrier, inc=1, device_id=to, device_id_type=MESH)

    def greet_plane(k, carry):
        greet(device(where_is(k)))
        return carry

    greet(other)
    for k in range(1, NY):
        greet(along_y(k))
    lax.fori_loop(1, XZ, greet_plane, 0)

    with jax.named_scope("logits"):
        par_copy.wait()

        def logits_step(i, peak):
            tok_copy(i).wait()
            rows = pl.ds(pl.multiple_of(i * TCH, TCH), TCH)
            block = dot(tok[rows, :], par[...])
            logits[rows, :] = block
            return jnp.maximum(peak, jnp.max(block, axis=0, keepdims=True))

        peak = lax.fori_loop(0, NT, logits_step, jnp.full((1, S), -jnp.inf, F32))
        win_copy = pltpu.make_async_copy(win_hbm, win, w_sem.at[0])
        wout_copy = pltpu.make_async_copy(wout_hbm, wout, w_sem.at[1])
        win_copy.start()
        wout_copy.start()

    with jax.named_scope("exps"):

        def weigh(i, total):
            rows = pl.ds(pl.multiple_of(i * 256, 256), 256)
            w = jnp.exp(logits[rows, :] - peak)
            disp_t[:, rows] = jnp.transpose(w).astype(BF16)
            return total + jnp.sum(w, axis=0, keepdims=True)

        total = lax.fori_loop(0, TOK // 256, weigh, jnp.zeros((1, S), F32))
        row8 = lax.broadcasted_iota(jnp.int32, (8, S), 0)
        core_own[...] = jnp.where(row8 == 0, peak, total)

    with jax.named_scope("barrier"):
        pl.semaphore_wait(barrier, XZ - 1 + NY - 1 + 1)
        core_copy = remote(core_own, core_other, core_s, core_r, other)
        core_copy.start()

    def part_copy(c):
        return remote(give.at[c], part.at[c], part_s.at[c], part_r.at[c], other)

    def targets(c):
        return ((x + 1) % NX, (x + 2) % NX) if c == 0 else ((x + 3) % NX, x)

    def matmul_step(c):
        group = S // NX
        lhs = jnp.concatenate(
            [disp_t[pl.ds(pl.multiple_of(tx * group, group), group), :] for tx in targets(c)], axis=0
        )
        block = dot(lhs, tok[...]).reshape(2, NZ, NC, ROWS, D)
        own[c] = jnp.where(core == 0, block[:, :, 0], block[:, :, 1])
        give[c] = jnp.where(core == 0, block[:, :, 1], block[:, :, 0]).astype(BF16)
        part_copy(c).start()

    with jax.named_scope("mm0"):
        matmul_step(0)

    with jax.named_scope("stats"):
        core_copy.wait()
        peak_o, total_o = core_other[0:1, :], core_other[1:2, :]
        chip_peak = jnp.maximum(peak, peak_o)
        f_own, f_other = jnp.exp(peak - chip_peak), jnp.exp(peak_o - chip_peak)
        chip_total = f_own * total + f_other * total_o
        turned = jnp.transpose(
            jnp.concatenate(
                [jnp.broadcast_to(v, (32, S)) for v in (f_own, f_other, chip_peak, chip_total)], axis=0
            )
        ).reshape(S // ROWS, ROWS, 128)
        lane = lax.broadcasted_iota(jnp.int32, (S // ROWS, ROWS, 128), 2)
        row = lax.broadcasted_iota(jnp.int32, (S // ROWS, ROWS, 128), 1)
        packed = jnp.where(lane == row, turned[:, :, 64:65], 0.0)
        packed = packed + jnp.where(lane == row + ROWS, turned[:, :, 96:97], 0.0)
        stats[...] = jnp.sum(packed, axis=1, keepdims=True)
        turned = turned.reshape(NX, NZ, NC, ROWS, 128)
        factors = jnp.where(core == 0, turned[:, :, 0], turned[:, :, 1])
        outb_f = factors

        def send_stats(k, carry):
            to_xz = where_is(k)
            remote(
                stats.at[to_xz * NC + core], stats_recv.at[xz], st_s, st_r, device(to_xz)
            ).start()
            return carry

        lax.fori_loop(1, XZ, send_stats, 0)
        stats_recv[xz] = stats[wide]

    with jax.named_scope("mm1"):
        matmul_step(1)

    def pick(tx):
        f = outb_f[0]
        for n in range(1, NX):
            f = jnp.where(tx == n, outb_f[n], f)
        return f

    def send_step(c):
        part_copy(c).wait()
        for h, tx in enumerate(targets(c)):
            f = pick(tx)
            outb[c, h] = (
                f[:, :, 0:1] * own[c, h] + f[:, :, 32:33] * part[c, h].astype(F32)
            ).astype(BF16)
        for h, tx in enumerate(targets(c)):
            for dz in range(NZ):
                tz = (z + dz) % NZ
                if c == 1 and h == 1 and dz == 0:
                    recv[xz] = outb[c, h, z]
                else:
                    remote(outb.at[c, h, tz], recv.at[xz], sc_s, sc_r, device(tx * NZ + tz)).start()

    def soften(i, carry):
        rows = pl.ds(pl.multiple_of(i * 256, 256), 256)
        block = logits[rows, :]
        e = jnp.exp(block - jnp.max(block, axis=1, keepdims=True))
        comb[rows, :] = (e / jnp.sum(e, axis=1, keepdims=True)).astype(BF16)
        return carry

    with jax.named_scope("send0"):
        send_step(0)
    with jax.named_scope("soft0"):
        lax.fori_loop(0, 3, soften, 0)
    with jax.named_scope("send1"):
        send_step(1)
    with jax.named_scope("soft1"):
        lax.fori_loop(3, TOK // 256, soften, 0)

    with jax.named_scope("scwait"):
        drain(stats_recv.at[pl.ds(0, XZ - 1)], st_r)
        drain(recv.at[pl.ds(0, XZ - 1)], sc_r)

    with jax.named_scope("reduce"):
        got = stats_recv[...].reshape(XZ, 128)
        top = jnp.max(got, axis=0, keepdims=True)
        factor = jnp.exp(jnp.minimum(got - top, 0.0))
        scaled = factor * pltpu.roll(got, 128 - ROWS, 1)
        flipped = jnp.transpose(
            jnp.concatenate([factor, scaled, jnp.broadcast_to(top, (128 - 2 * XZ, 128))], axis=0)
        )[0:ROWS, :]
        acc = jnp.zeros((ROWS, D), F32)
        for q in range(XZ):
            acc = acc + flipped[:, q : q + 1] * recv[q].astype(F32)
        plane_total = jnp.sum(flipped[:, XZ : 2 * XZ], axis=1, keepdims=True)
        ybuf[y] = acc.astype(BF16)
        lane2 = lax.broadcasted_iota(jnp.int32, (ROWS, 128), 1)
        ystat[y] = jnp.where(lane2 < 64, flipped[:, 2 * XZ : 2 * XZ + 1], plane_total)

    def y_copy(k):
        return remote(ybuf.at[y], ybuf.at[y], y_s.at[k - 1], y_r.at[k - 1], along_y(k))

    def ystat_copy(k):
        return remote(ystat.at[y], ystat.at[y], yst_s.at[k - 1], yst_r.at[k - 1], along_y(k))

    with jax.named_scope("yex"):
        for k in (2, 1, 3):
            ystat_copy(k).start()
            y_copy(k).start()
        win_copy.wait()
        wout_copy.wait()
        for k in range(1, NY):
            ystat_copy(k).wait()
            y_copy(k).wait()

    with jax.named_scope("ffn"):
        tops = [ystat[n][:, 0:1] for n in range(NY)]
        gmax = jnp.maximum(jnp.maximum(tops[0], tops[1]), jnp.maximum(tops[2], tops[3]))
        grand = jnp.zeros((ROWS, 1), F32)
        acc = jnp.zeros((ROWS, D), F32)
        for n in range(NY):
            f = jnp.exp(tops[n] - gmax)
            grand = grand + f * ystat[n][:, 64:65]
            acc = acc + f * ybuf[n].astype(F32)
        slot_in = (acc / grand).astype(BF16)
        expert = lax.broadcasted_iota(jnp.int32, (ROWS, H), 0) // 4
        hidden = jnp.zeros((ROWS, H), F32)
        for e in range(4):
            hidden = jnp.where(expert == e, dot(slot_in, win[e]), hidden)
        hidden = jax.nn.gelu(hidden).astype(BF16).astype(F32)
        total_out = jnp.zeros((ROWS, D), F32)
        for e in range(4):
            total_out = total_out + dot(jnp.where(expert == e, hidden, 0.0).astype(BF16), wout[e])
        obuf[y] = total_out

    def o_copy(k):
        return remote(obuf.at[y], obuf.at[y], o_s.at[k - 1], o_r.at[k - 1], along_y(k))

    with jax.named_scope("oex"):
        for k in (2, 1, 3):
            o_copy(k).start()
        for k in range(1, NY):
            o_copy(k).wait()

    def half(h):
        return slice(h * HALF, (h + 1) * HALF)

    def spread(h, k):
        block = so.at[xz, core, :, half(h)]
        return remote(block, block, ag_s, ag_r.at[h, k // NZ], device(where_is(k)))

    def forward(h, dx):
        fx = (x - dx + NX) % NX
        block = so.at[pl.ds(fx * NZ, NZ), core, :, half(h)]
        return remote(block, block, fw_s.at[h, dx], fw_r.at[h, dx], other)

    with jax.named_scope("spread"):
        so[xz, core] = (obuf[0] + obuf[1] + obuf[2] + obuf[3]).astype(BF16)
        for h in range(2):
            for k in range(1, XZ):
                spread(h, k).start()

    for h in range(2):
        with jax.named_scope("agwait"):
            for dx in range(NX):
                n = NZ - (1 if dx == 0 else 0)
                drain(so.at[pl.ds(0, n), 0, :, half(h)], ag_r.at[h, dx])
                forward(h, dx).start()
            for dx in range(NX):
                forward(h, dx).wait()
        with jax.named_scope("mix"):

            def mix(i, carry):
                rows = pl.ds(pl.multiple_of(i * TCH, TCH), TCH)
                table = so[:, :, :, half(h)].reshape(S, HALF)
                out[rows, half(h)] = dot(comb[rows, :], table).astype(BF16)
                return carry

            lax.fori_loop(0, NT, mix, 0)

    drain(stats_recv.at[pl.ds(0, XZ - 1)], st_s)
    drain(recv.at[pl.ds(0, XZ - 1)], sc_s)
    drain(recv.at[pl.ds(0, XZ - 1)], ag_s)


def shards(tokens, slot_params, expert_in, expert_out):
    dma, vmem = pltpu.SemaphoreType.DMA, pltpu.VMEM
    return pl.pallas_call(
        layer_kernel,
        out_shape=pltpu.VMEM((TOK, D), BF16),
        in_specs=[pl.BlockSpec(memory_space=pltpu.HBM)] * 4,
        out_specs=pl.BlockSpec(memory_space=pltpu.VMEM),
        scratch_shapes=[
            vmem((TOK, D), BF16),
            vmem((D, S), BF16),
            vmem((4, D, H), BF16),
            vmem((4, H, D), BF16),
            vmem((TOK, S), F32),
            vmem((S, TOK), BF16),
            vmem((TOK, S), BF16),
            vmem((2, 2, NZ, ROWS, D), F32),
            vmem((2, 2, NZ, ROWS, D), BF16),
            vmem((2, 2, NZ, ROWS, D), BF16),
            vmem((2, 2, NZ, ROWS, D), BF16),
            vmem((XZ, ROWS, D), BF16),
            vmem((8, S), F32),
            vmem((8, S), F32),
            vmem((S // ROWS, 1, 128), F32),
            vmem((XZ, 1, 128), F32),
            vmem((NY, ROWS, D), BF16),
            vmem((NY, ROWS, 128), F32),
            vmem((NY, ROWS, D), F32),
            vmem((XZ, NC, ROWS, D), BF16),
            dma((NT + 1,)),
            dma((2,)),
            dma, dma,
            dma((2,)), dma((2,)),
            dma, dma, dma, dma,
            dma((NY - 1,)), dma((NY - 1,)),
            dma((NY - 1,)), dma((NY - 1,)),
            dma((NY - 1,)), dma((NY - 1,)),
            dma, dma((2, NX)),
            dma((2, NX)), dma((2, NX)),
        ],
        compiler_params=pltpu.CompilerParams(
            collective_id=0, has_side_effects=True, vmem_limit_bytes=50331648
        ),
        name="layer",
    )(*[pltpu.with_memory_space_constraint(v, pltpu.HBM) for v in (tokens, slot_params, expert_in, expert_out)])


def solution(mesh):
    return jax.shard_map(
        shards,
        mesh=mesh,
        in_specs=(
            P(("wide", "narrow"), None),
            P(),
            P("wide", None, "narrow"),
            P("wide", "narrow", None),
        ),
        out_specs=P(("wide", "narrow"), None),
        check_vma=False,
    )
```

time: 313 us -> 49.7 us (0.16)
  blocking collectives: 147 us -> 0 us
  waiting for transfers between devices: 118 us -> 0 us
  Pallas kernels: 0 us -> 47.6 us
  matrix products: 28.7 us -> 0 us
  between operations: 13.1 us -> 0.01 us
  other arithmetic: 4.06 us -> 0 us
    psum x2 -> x0, blocking collectives: 78.6 us -> none  [the longest x1 66 us: shards(): slot_totals = lax.psum(jnp.sum(weights, axis=0), ('wide', 'narrow'))]
    reduce_scatter x1 -> x0, waiting for transfers between devices: 73.9 us -> none  [shards(): lax.psum_scatter(lax.dot_general(columns, tokens, (((0,), (0,)), ((), ())...]
    pmax x1 -> x0, blocking collectives: 68.6 us -> none  [shards(): column_peak = lax.pmax(local_peak, ('wide', 'narrow'))]
    pallas_call x0 -> x1, Pallas kernels: none -> 47.6 us  [shards(): pl.pallas_call(layer_kernel, out_shape=pltpu.VMEM((TOK, D), BF16), in_spe...]
    all_gather x1 -> x0, waiting for transfers between devices: 43.9 us -> none  [shards(): lax.all_gather(whole_rows, 'wide', axis=0, tiled=True)]
    dot_general x4 -> x0, matrix products: 28.7 us -> none  [the longest x1 8.04 us: shards(): jnp.einsum('esh,ehd->esd', hidden, expert_out, preferred_element_type=jnp...]
    reduce_sum x1 -> x0, other arithmetic: 3.15 us -> none  [shards(): mixing = jax.nn.softmax(logits, axis=1).astype(jnp.bfloat16)]
  transfers between devices with their start and end apart: 3 -> 0, of which waited for: 2 -> 0; matrix products, arithmetic and copies ran while one was open for 1% -> 0% of each run, Pallas kernels for 0% -> 0%
where the time goes in v2:
time: 49.7 us; the launch traced here: 49.6 us
  Pallas kernels  47.6 us (96%)
  local copies, waits for them, and re-layouts  2.02 us (4%)
    pallas_call x1, Pallas kernels, shards(): pl.pallas_call(layer_kernel, out_shape=pltpu.VMEM((TOK, D), BF16), in_spe...  47.6 us
    unnamed x1, local copies, waits for them, and re-layouts  2.02 us

profile of v2, /device:TPU:1, one launch (start us, length us, event | category | flops | bytes accessed | tf_op | source)
XLA Modules:
  0.0 49.6 jit_solution(826470428669634264)
XLA Ops:
  0.0 47.6 %layer.1 = bf16[2048,1024]{1,0:T(8,128)(2,1)S(1)} custom-call(bf16[2048,1024]{1,0:T(8,128)(2,1)} %tok_hbm.1, bf16[1024,512]{1,0:T(8,128)(2,1)} %par_hbm.1, bf16[4,1024,1024]{2,1,0:T(8,128)(2,1)} %win_hbm.1, bf16[4,1024,1024]{2,1,0:T(8,128)(2,1)} %wout_hbm.1), custom_call_target="tpu_custom_call" | custom-call | tf_op jit(solution)/shard_map/layer/pallas_call | solution.py:310
  47.6 2.0 %copy.6 = bf16[2048,1024]{1,0:T(8,128)(2,1)} copy(bf16[2048,1024]{1,0:T(8,128)(2,1)S(1)} %layer.1) | data formatting | bytes 8388608

commit v3 on v2

v3 whole, which is shorter than its diff:
```python
import jax
import jax.numpy as jnp
from jax import lax
from jax.experimental import pallas as pl
from jax.experimental.pallas import tpu as pltpu
from jax.sharding import PartitionSpec as P

MESH = pl.DeviceIdType.MESH
F32, BF16 = jnp.float32, jnp.bfloat16
NX, NZ, NY, NC = 4, 4, 4, 2
XZ = NX * NZ
ROWS = 16
PIPE = 2
PR = ROWS // PIPE
TOK, D, S, H = 2048, 1024, 512, 1024
SP = S // PIPE
TCH = 512
NT = TOK // TCH
SOFT = 256


def dot(a, b):
    return jnp.dot(a, b, preferred_element_type=F32)


def layer_kernel(
    tok_hbm, par_hbm, win_hbm, wout_hbm, mixed, comb, last,
    tok, par, win, wout, logits, disp_t, order, own, give, part, outb, recv,
    core_own, core_other, stats, stats_recv, ystat, ybuf, obuf, so, first,
    in_sem, w_sem, core_s, core_r, part_s, part_r, st_s, st_r, sc_s, sc_r,
    yst_s, yst_r, y_s, y_r, o_s, o_r, ag_s, ag_r, fw_s, fw_r,
):
    wide = lax.axis_index("wide")
    y = lax.axis_index("narrow")
    core = wide % NC
    xz = wide // NC
    x, z = xz // NZ, xz % NZ

    def where_is(k):
        dx, dz = k // NZ, k % NZ
        return ((x + dx) % NX) * NZ + (z + dz) % NZ

    def device(to_xz):
        return {"wide": to_xz * NC + core, "narrow": y}

    def along_y(k):
        return {"wide": wide, "narrow": (y + k) % NY}

    other = {"wide": xz * NC + 1 - core, "narrow": y}

    def remote(src, dst, send, recv_sem, to):
        return pltpu.make_async_remote_copy(
            src_ref=src, dst_ref=dst, send_sem=send, recv_sem=recv_sem,
            device_id=to, device_id_type=MESH,
        )

    def drain(ref, sem):
        pltpu.make_async_copy(ref, ref, sem).wait()

    def tok_copy(i):
        rows = pl.ds(i * TCH, TCH)
        return pltpu.make_async_copy(tok_hbm.at[rows], tok.at[rows], in_sem.at[i])

    par_copy = pltpu.make_async_copy(par_hbm, par, in_sem.at[NT])
    par_copy.start()
    tok_copy(0).start()

    barrier = pltpu.get_barrier_semaphore()

    def greet(to):
        pl.semaphore_signal(barrier, inc=1, device_id=to, device_id_type=MESH)

    def greet_plane(k, carry):
        greet(device(where_is(k)))
        return carry

    greet(other)
    for k in range(1, NY):
        greet(along_y(k))
    lax.fori_loop(1, XZ, greet_plane, 0)
    for i in range(1, NT):
        tok_copy(i).start()

    with jax.named_scope("logits"):
        par_copy.wait()

        def logits_step(i, peak):
            tok_copy(i).wait()
            rows = pl.ds(pl.multiple_of(i * TCH, TCH), TCH)
            block = dot(tok[rows, :], par[...])
            logits[rows, :] = block
            return jnp.maximum(peak, jnp.max(block, axis=0, keepdims=True))

        peak = lax.fori_loop(0, NT, logits_step, jnp.full((1, S), -jnp.inf, F32))
        win_copy = pltpu.make_async_copy(win_hbm, win, w_sem.at[0])
        wout_copy = pltpu.make_async_copy(wout_hbm, wout, w_sem.at[1])
        win_copy.start()
        wout_copy.start()

    with jax.named_scope("exps"):

        def weigh(i, total):
            rows = pl.ds(pl.multiple_of(i * 256, 256), 256)
            w = jnp.exp(logits[rows, :] - peak)
            turned = jnp.transpose(w).reshape(S // ROWS, PIPE, PR, 256)
            for p in range(PIPE):
                disp_t[p, :, rows] = turned[:, p].reshape(SP, 256).astype(BF16)
            return total + jnp.sum(w, axis=0, keepdims=True)

        total = lax.fori_loop(0, TOK // 256, weigh, jnp.zeros((1, S), F32))
        row8 = lax.broadcasted_iota(jnp.int32, (8, S), 0)
        core_own[...] = jnp.where(row8 == 0, peak, total)

    with jax.named_scope("barrier"):
        pl.semaphore_wait(barrier, XZ - 1 + NY - 1 + 1)
        core_copy = remote(core_own, core_other, core_s, core_r, other)
        core_copy.start()

    def part_copy(p):
        return remote(give.at[p], part.at[p], part_s.at[p], part_r.at[p], other)

    def matmul_step(p):
        block = dot(disp_t[p], tok[...]).reshape(XZ, NC, PR, D)
        own[p] = jnp.where(core == 0, block[:, 0], block[:, 1])
        give[p] = jnp.where(core == 0, block[:, 1], block[:, 0]).astype(BF16)
        part_copy(p).start()

    with jax.named_scope("mm0"):
        matmul_step(0)

    with jax.named_scope("stats"):
        core_copy.wait()
        peak_o, total_o = core_other[0:1, :], core_other[1:2, :]
        chip_peak = jnp.maximum(peak, peak_o)
        f_own, f_other = jnp.exp(peak - chip_peak), jnp.exp(peak_o - chip_peak)
        chip_total = f_own * total + f_other * total_o
        turned = jnp.transpose(
            jnp.concatenate(
                [jnp.broadcast_to(v, (32, S)) for v in (f_own, f_other, chip_peak, chip_total)], axis=0
            )
        ).reshape(S // ROWS, ROWS, 128)
        lane = lax.broadcasted_iota(jnp.int32, (S // ROWS, ROWS, 128), 2)
        row = lax.broadcasted_iota(jnp.int32, (S // ROWS, ROWS, 128), 1)
        packed = jnp.where(lane == row, turned[:, :, 64:65], 0.0)
        packed = packed + jnp.where(lane == row + ROWS, turned[:, :, 96:97], 0.0)
        stats[...] = jnp.sum(packed, axis=1, keepdims=True)
        turned = turned.reshape(XZ, NC, ROWS, 128)
        factors = jnp.where(core == 0, turned[:, 0], turned[:, 1])

        def send_stats(k, carry):
            to_xz = where_is(k)
            remote(
                stats.at[to_xz * NC + core], stats_recv.at[xz], st_s, st_r, device(to_xz)
            ).start()
            return carry

        lax.fori_loop(1, XZ, send_stats, 0)
        stats_recv[xz] = stats[wide]

    with jax.named_scope("mm1"):
        matmul_step(1)

    def send_step(p):
        part_copy(p).wait()
        f = factors[:, p * PR : (p + 1) * PR]
        outb[p] = (f[:, :, 0:1] * own[p] + f[:, :, 32:33] * part[p].astype(F32)).astype(BF16)

        def send(k, carry):
            to_xz = where_is(k)
            remote(outb.at[p, to_xz], recv.at[p, xz], sc_s.at[p], sc_r.at[p], device(to_xz)).start()
            return carry

        lax.fori_loop(1, XZ, send, 0)
        recv[p, xz] = outb[p, xz]

    def soften(i, carry):
        rows = pl.ds(pl.multiple_of(i * SOFT, SOFT), SOFT)
        block = logits[rows, :]
        e = jnp.exp(block - jnp.max(block, axis=1, keepdims=True))
        share = (e / jnp.sum(e, axis=1, keepdims=True)).astype(BF16)
        comb[rows, :] = dot(share, order[...]).astype(BF16)
        return carry

    with jax.named_scope("send0"):
        send_step(0)
    with jax.named_scope("soft0"):
        new = lax.broadcasted_iota(jnp.int32, (S, S), 1)
        old = lax.broadcasted_iota(jnp.int32, (S, S), 0)
        within = new % SP
        source = (within // PR) * ROWS + (new // SP) * PR + within % PR
        order[...] = jnp.where(old == source, 1.0, 0.0).astype(BF16)
        lax.fori_loop(0, 1, soften, 0)
    with jax.named_scope("send1"):
        send_step(1)
    with jax.named_scope("soft1"):
        lax.fori_loop(1, 5, soften, 0)

    with jax.named_scope("ystat"):
        drain(stats_recv.at[pl.ds(0, XZ - 1)], st_r)
        got = stats_recv[...].reshape(XZ, 128)
        top = jnp.max(got, axis=0, keepdims=True)
        factor = jnp.exp(jnp.minimum(got - top, 0.0))
        scaled = factor * pltpu.roll(got, 128 - ROWS, 1)
        flipped = jnp.transpose(
            jnp.concatenate([factor, scaled, jnp.broadcast_to(top, (128 - 2 * XZ, 128))], axis=0)
        )[0:ROWS, :]
        plane_top = flipped[:, 2 * XZ : 2 * XZ + 1]
        plane_total = jnp.sum(flipped[:, XZ : 2 * XZ], axis=1, keepdims=True)
        lane2 = lax.broadcasted_iota(jnp.int32, (ROWS, 128), 1)
        ystat[y] = jnp.where(lane2 < 64, plane_top, plane_total)

        def ystat_copy(k):
            return remote(ystat.at[y], ystat.at[y], yst_s.at[k - 1], yst_r.at[k - 1], along_y(k))

        for k in (2, 1, 3):
            ystat_copy(k).start()

    with jax.named_scope("soft2"):
        lax.fori_loop(5, TOK // SOFT, soften, 0)

    with jax.named_scope("ystatw"):
        for k in range(1, NY):
            ystat_copy(k).wait()
        tops = [ystat[n][:, 0:1] for n in range(NY)]
        all_top = jnp.maximum(jnp.maximum(tops[0], tops[1]), jnp.maximum(tops[2], tops[3]))
        grand = jnp.zeros((ROWS, 1), F32)
        for n in range(NY):
            grand = grand + jnp.exp(tops[n] - all_top) * ystat[n][:, 64:65]
        scale = jnp.exp(plane_top - all_top) / grand

    def y_copy(p, k):
        return remote(
            ybuf.at[p, y], ybuf.at[p, y], y_s.at[p, k - 1], y_r.at[p, k - 1], along_y(k)
        )

    def o_copy(p, k):
        return remote(
            obuf.at[p, y], obuf.at[p, y], o_s.at[p, k - 1], o_r.at[p, k - 1], along_y(k)
        )

    for p in range(PIPE):
        with jax.named_scope("scwait"):
            drain(recv.at[p, pl.ds(0, XZ - 1)], sc_r.at[p])
        with jax.named_scope("reduce"):
            mine = slice(p * PR, (p + 1) * PR)
            acc = jnp.zeros((PR, D), F32)
            for q in range(XZ):
                acc = acc + flipped[mine, q : q + 1] * recv[p, q].astype(F32)
            ybuf[p, y] = (acc * scale[mine]).astype(BF16)
            for k in (2, 1, 3):
                y_copy(p, k).start()

    win_copy.wait()
    wout_copy.wait()
    per = PR // 4
    expert = lax.broadcasted_iota(jnp.int32, (PR, H), 0) // 4
    for p in range(PIPE):
        with jax.named_scope("yex"):
            for k in range(1, NY):
                y_copy(p, k).wait()
        with jax.named_scope("ffn"):
            slot_in = jnp.sum(ybuf[p].astype(F32), axis=0).astype(BF16)
            hidden = jnp.zeros((PR, H), F32)
            for e in range(per):
                hidden = jnp.where(expert == e, dot(slot_in, win[p * per + e]), hidden)
            hidden = jax.nn.gelu(hidden).astype(BF16).astype(F32)
            result = jnp.zeros((PR, D), F32)
            for e in range(per):
                result = result + dot(
                    jnp.where(expert == e, hidden, 0.0).astype(BF16), wout[p * per + e]
                )
            obuf[p, y] = result
            for k in (2, 1, 3):
                o_copy(p, k).start()

    def spread(p, k):
        block = so.at[p, xz, core]
        return remote(block, block, ag_s.at[p], ag_r.at[p, k // NZ], device(where_is(k)))

    def forward(p, dx):
        fx = (x - dx + NX) % NX
        block = so.at[p, pl.ds(fx * NZ, NZ), core]
        return remote(block, block, fw_s.at[p, dx], fw_r.at[p, dx], other)

    def arrive(p, dx):
        n = NZ - (1 if dx == 0 else 0)
        drain(so.at[p, pl.ds(0, n), 0], ag_r.at[p, dx])
        forward(p, dx).start()

    for p in range(PIPE):
        with jax.named_scope("oex"):
            for k in range(1, NY):
                o_copy(p, k).wait()
        with jax.named_scope("spread"):
            so[p, xz, core] = (obuf[p, 0] + obuf[p, 1] + obuf[p, 2] + obuf[p, 3]).astype(BF16)

            def send_out(k, carry):
                spread(p, k).start()
                return carry

            lax.fori_loop(1, XZ, send_out, 0)

    def mix(i):
        rows = pl.ds(pl.multiple_of(i * TCH, TCH), TCH)
        mixed[rows, :] = dot(comb[rows, 0:SP], first[...])

    with jax.named_scope("agA"):
        for dx in (0, 1, 3, 2):
            arrive(0, dx)
        for dx in range(NX):
            forward(0, dx).wait()
        first[...] = so[0].reshape(SP, D)
    with jax.named_scope("mixA"):
        for i, dx in enumerate((0, 1, 3, 2)):
            mix(i)
            arrive(1, dx)
    with jax.named_scope("agB"):
        for dx in range(NX):
            forward(1, dx).wait()
        last[...] = so[1].reshape(SP, D)

    drain(stats_recv.at[pl.ds(0, XZ - 1)], st_s)
    for p in range(PIPE):
        drain(recv.at[p, pl.ds(0, XZ - 1)], sc_s.at[p])
        drain(recv.at[p, pl.ds(0, XZ - 1)], ag_s.at[p])


def finish_kernel(mixed, comb, last, out, stage, sems):
    def out_copy(i):
        rows = pl.ds(i * SOFT, SOFT)
        return pltpu.make_async_copy(stage.at[rows], out.at[rows], sems.at[i])

    for i in range(TOK // SOFT):
        rows = pl.ds(i * SOFT, SOFT)
        stage[rows, :] = (mixed[rows, :] + dot(comb[rows, SP:S], last[...])).astype(BF16)
        out_copy(i).start()
    for i in range(TOK // SOFT):
        out_copy(i).wait()


def shards(tokens, slot_params, expert_in, expert_out):
    dma, vmem = pltpu.SemaphoreType.DMA, pltpu.VMEM
    operands = [
        pltpu.with_memory_space_constraint(v, pltpu.HBM)
        for v in (tokens, slot_params, expert_in, expert_out)
    ]
    held = pl.pallas_call(
        layer_kernel,
        out_shape=(vmem((TOK, D), F32), vmem((TOK, S), BF16), vmem((SP, D), BF16)),
        in_specs=[pl.BlockSpec(memory_space=pltpu.HBM)] * 4,
        out_specs=[pl.BlockSpec(memory_space=pltpu.VMEM)] * 3,
        scratch_shapes=[
            vmem((TOK, D), BF16),
            vmem((D, S), BF16),
            vmem((4, D, H), BF16),
            vmem((4, H, D), BF16),
            vmem((TOK, S), F32),
            vmem((PIPE, SP, TOK), BF16),
            vmem((S, S), BF16),
            vmem((PIPE, XZ, PR, D), F32),
            vmem((PIPE, XZ, PR, D), BF16),
            vmem((PIPE, XZ, PR, D), BF16),
            vmem((PIPE, XZ, PR, D), BF16),
            vmem((PIPE, XZ, PR, D), BF16),
            vmem((8, S), F32),
            vmem((8, S), F32),
            vmem((S // ROWS, 1, 128), F32),
            vmem((XZ, 1, 128), F32),
            vmem((NY, ROWS, 128), F32),
            vmem((PIPE, NY, PR, D), BF16),
            vmem((PIPE, NY, PR, D), F32),
            vmem((PIPE, XZ, NC, PR, D), BF16),
            vmem((SP, D), BF16),
            dma((NT + 1,)),
            dma((2,)),
            dma, dma,
            dma((PIPE,)), dma((PIPE,)),
            dma, dma,
            dma((PIPE,)), dma((PIPE,)),
            dma((NY - 1,)), dma((NY - 1,)),
            dma((PIPE, NY - 1)), dma((PIPE, NY - 1)),
            dma((PIPE, NY - 1)), dma((PIPE, NY - 1)),
            dma((PIPE,)), dma((PIPE, NX)),
            dma((PIPE, NX)), dma((PIPE, NX)),
        ],
        compiler_params=pltpu.CompilerParams(
            collective_id=0, has_side_effects=True, vmem_limit_bytes=48 * 1024 * 1024
        ),
        name="layer",
    )(*operands)
    return pl.pallas_call(
        finish_kernel,
        out_shape=jax.ShapeDtypeStruct((TOK, D), BF16),
        in_specs=[pl.BlockSpec(memory_space=pltpu.VMEM)] * 3,
        out_specs=pl.BlockSpec(memory_space=pl.ANY),
        scratch_shapes=[vmem((TOK, D), BF16), dma((TOK // SOFT,))],
        compiler_params=pltpu.CompilerParams(vmem_limit_bytes=32 * 1024 * 1024),
        name="finish",
    )(*held)


def solution(mesh):
    return jax.shard_map(
        shards,
        mesh=mesh,
        in_specs=(
            P(("wide", "narrow"), None),
            P(),
            P("wide", None, "narrow"),
            P("wide", "narrow", None),
        ),
        out_specs=P(("wide", "narrow"), None),
        check_vma=False,
    )
```

time: 49.7 us -> 44.6 us (0.90)
  Pallas kernels: 47.6 us -> 44.4 us
  local copies, waits for them, and re-layouts: 2.02 us -> 0 us
    pallas_call x1 -> x2, Pallas kernels: 47.6 us -> 44.4 us  [the longest x1 42.1 us: shards(): pl.pallas_call(layer_kernel, out_shape=(vmem((TOK, D), F32), vmem((TOK, S...]
    unnamed x1 -> x0, local copies, waits for them, and re-layouts: 2.02 us -> none
where the time goes in v3:
time: 44.6 us; the launch traced here: 44.5 us
  Pallas kernels  44.4 us (100%)
    pallas_call x1, Pallas kernels, shards(): pl.pallas_call(layer_kernel, out_shape=(vmem((TOK, D), F32), vmem((TOK, S...  42.1 us
    pallas_call x1, Pallas kernels, shards(): pl.pallas_call(finish_kernel, out_shape=jax.ShapeDtypeStruct((TOK, D), BF...  2.38 us

profile of v3, /device:TPU:1, one launch (start us, length us, event | category | flops | bytes accessed | tf_op | source)
XLA Modules:
  0.0 44.5 jit_solution(10477117594537609711)
XLA Ops:
  0.0 42.1 %layer.1 = (f32[2048,1024]{1,0:T(8,128)S(1)}, bf16[2048,512]{1,0:T(8,128)(2,1)S(1)}, bf16[256,1024]{1,0:T(8,128)(2,1)S(1)}) custom-call(bf16[2048,1024]{1,0:T(8,128)(2,1)} %tok_hbm.1, bf16[1024,512]{1,0:T(8,128)(2,1)} %par_hbm.1, bf16[4,1024,1024]{2,1,0:T(8,128)(2,1)} %win_hbm.1, bf16[4,1024,1024]{2,1,0:T(8,128)(2,1)} %wout_hbm.1), custom_call_target="tpu_custom_call" | custom-call | tf_op jit(solution)/shard_map/layer/pallas_call | solution.py:347
  42.1 2.4 %finish.1 = bf16[2048,1024]{1,0:T(8,128)(2,1)} custom-call(f32[2048,1024]{1,0:T(8,128)S(1)} %get-tuple-element.8.mixed, bf16[2048,512]{1,0:T(8,128)(2,1)S(1)} %get-tuple-element.9.comb, bf16[256,1024]{1,0:T(8,128)(2,1)S(1)} %get-tuple-element.10.last), custom_call_target="tpu_custom_call" | custom-call | tf_op jit(solution)/shard_map/finish/pallas_call | solution.py:391

commit v4 on v3

--- a/solution.py
+++ b/solution.py
@@ -10,12 +10,16 @@
 NX, NZ, NY, NC = 4, 4, 4, 2
 XZ = NX * NZ
 ROWS = 16
-PIPE = 2
+PIPE = 4
 PR = ROWS // PIPE
+PH = PIPE // 2
+HR = ROWS // 2
 TOK, D, S, H = 2048, 1024, 512, 1024
 SP = S // PIPE
+SH = S // 2
 TCH = 512
 NT = TOK // TCH
+MCH = 512
 SOFT = 256
 
 
@@ -97,17 +101,23 @@
         win_copy.start()
         wout_copy.start()
 
+    def weigh(i):
+        rows = pl.ds(i * MCH, MCH)
+        w = jnp.exp(logits[rows, :] - peak)
+        turned = jnp.transpose(w).reshape(S // ROWS, 2, HR, MCH)
+        for h in range(2):
+            disp_t[h, :, rows] = turned[:, h].reshape(SH, MCH).astype(BF16)
+        return jnp.sum(w, axis=0, keepdims=True)
+
     with jax.named_scope("exps"):
-
-        def weigh(i, total):
-            rows = pl.ds(pl.multiple_of(i * 256, 256), 256)
-            w = jnp.exp(logits[rows, :] - peak)
-            turned = jnp.transpose(w).reshape(S // ROWS, PIPE, PR, 256)
-            for p in range(PIPE):
-                disp_t[p, :, rows] = turned[:, p].reshape(SP, 256).astype(BF16)
-            return total + jnp.sum(w, axis=0, keepdims=True)
-
-        total = lax.fori_loop(0, TOK // 256, weigh, jnp.zeros((1, S), F32))
+        total = weigh(0)
+        block = None
+        for i in range(TOK // MCH):
+            rows = pl.ds(i * MCH, MCH)
+            step = dot(disp_t[0, :, rows], tok[rows, :])
+            block = step if block is None else block + step
+            if i + 1 < TOK // MCH:
+                total = total + weigh(i + 1)
         row8 = lax.broadcasted_iota(jnp.int32, (8, S), 0)
         core_own[...] = jnp.where(row8 == 0, peak, total)
 
@@ -116,17 +126,20 @@
         core_copy = remote(core_own, core_other, core_s, core_r, other)
         core_copy.start()
 
-    def part_copy(p):
-        return remote(give.at[p], part.at[p], part_s.at[p], part_r.at[p], other)
-
-    def matmul_step(p):
-        block = dot(disp_t[p], tok[...]).reshape(XZ, NC, PR, D)
-        own[p] = jnp.where(core == 0, block[:, 0], block[:, 1])
-        give[p] = jnp.where(core == 0, block[:, 1], block[:, 0]).astype(BF16)
-        part_copy(p).start()
+    def part_copy(h):
+        return remote(give.at[h], part.at[h], part_s.at[h], part_r.at[h], other)
+
+    def share_block(h, block):
+        block = block.reshape(XZ, NC, HR, D)
+        own[h] = jnp.where(core == 0, block[:, 0], block[:, 1])
+        give[h] = jnp.where(core == 0, block[:, 1], block[:, 0]).astype(BF16)
+        part_copy(h).start()
 
     with jax.named_scope("mm0"):
-        matmul_step(0)
+        share_block(0, block)
+
+    with jax.named_scope("mm1"):
+        share_block(1, dot(disp_t[1], tok[...]))
 
     with jax.named_scope("stats"):
         core_copy.wait()
@@ -157,21 +170,23 @@
         lax.fori_loop(1, XZ, send_stats, 0)
         stats_recv[xz] = stats[wide]
 
-    with jax.named_scope("mm1"):
-        matmul_step(1)
-
-    def send_step(p):
-        part_copy(p).wait()
-        f = factors[:, p * PR : (p + 1) * PR]
-        outb[p] = (f[:, :, 0:1] * own[p] + f[:, :, 32:33] * part[p].astype(F32)).astype(BF16)
-
-        def send(k, carry):
-            to_xz = where_is(k)
-            remote(outb.at[p, to_xz], recv.at[p, xz], sc_s.at[p], sc_r.at[p], device(to_xz)).start()
-            return carry
-
-        lax.fori_loop(1, XZ, send, 0)
-        recv[p, xz] = outb[p, xz]
+    def send_step(h):
+        part_copy(h).wait()
+        f = factors[:, h * HR : (h + 1) * HR]
+        joined = (f[:, :, 0:1] * own[h] + f[:, :, 32:33] * part[h].astype(F32)).astype(BF16)
+        for p in range(h * PH, (h + 1) * PH):
+            outb[p] = joined[:, (p % PH) * PR : (p % PH + 1) * PR]
+        for p in range(h * PH, (h + 1) * PH):
+
+            def send(k, carry):
+                to_xz = where_is(k)
+                remote(
+                    outb.at[p, to_xz], recv.at[p, xz], sc_s.at[p], sc_r.at[p], device(to_xz)
+                ).start()
+                return carry
+
+            lax.fori_loop(1, XZ, send, 0)
+            recv[p, xz] = outb[p, xz]
 
     def soften(i, carry):
         rows = pl.ds(pl.multiple_of(i * SOFT, SOFT), SOFT)
@@ -193,7 +208,7 @@
     with jax.named_scope("send1"):
         send_step(1)
     with jax.named_scope("soft1"):
-        lax.fori_loop(1, 5, soften, 0)
+        lax.fori_loop(1, 3, soften, 0)
 
     with jax.named_scope("ystat"):
         drain(stats_recv.at[pl.ds(0, XZ - 1)], st_r)
@@ -216,62 +231,62 @@
             ystat_copy(k).start()
 
     with jax.named_scope("soft2"):
-        lax.fori_loop(5, TOK // SOFT, soften, 0)
-
+        lax.fori_loop(3, 4, soften, 0)
+
+    def y_copy(p, k):
+        return remote(
+            ybuf.at[p, y], ybuf.at[p, y], y_s.at[p, k - 1], y_r.at[p, k - 1], along_y(k)
+        )
+
+    def o_copy(p, k):
+        return remote(
+            obuf.at[p, y], obuf.at[p, y], o_s.at[p, k - 1], o_r.at[p, k - 1], along_y(k)
+        )
+
+    def gather(p):
+        with jax.named_scope(f"sc{p}"):
+            drain(recv.at[p, pl.ds(0, XZ - 1)], sc_r.at[p])
+            mine = slice(p * PR, (p + 1) * PR)
+            acc = jnp.zeros((PR, D), F32)
+            for q in range(XZ):
+                acc = acc + flipped[mine, q : q + 1] * recv[p, q].astype(F32)
+            ybuf[p, y] = acc.astype(BF16)
+            for k in (2, 1, 3):
+                y_copy(p, k).start()
+
+    def expert(p):
+        with jax.named_scope(f"ffn{p}"):
+            for k in range(1, NY):
+                y_copy(p, k).wait()
+            mine = slice(p * PR, (p + 1) * PR)
+            acc = jnp.zeros((PR, D), F32)
+            for n in range(NY):
+                acc = acc + scale[n][mine] * ybuf[p, n].astype(F32)
+            hidden = jax.nn.gelu(dot(acc.astype(BF16), win[p])).astype(BF16)
+            obuf[p, y] = dot(hidden, wout[p]).astype(BF16)
+            for k in (2, 1, 3):
+                o_copy(p, k).start()
+
+    def soft(i):
+        with jax.named_scope(f"soft{i}"):
+            soften(i, 0)
+
+    gather(0)
+    gather(1)
+    soft(4)
+    gather(2)
     with jax.named_scope("ystatw"):
+        win_copy.wait()
+        wout_copy.wait()
         for k in range(1, NY):
             ystat_copy(k).wait()
         tops = [ystat[n][:, 0:1] for n in range(NY)]
         all_top = jnp.maximum(jnp.maximum(tops[0], tops[1]), jnp.maximum(tops[2], tops[3]))
+        scale = [jnp.exp(tops[n] - all_top) for n in range(NY)]
         grand = jnp.zeros((ROWS, 1), F32)
         for n in range(NY):
-            grand = grand + jnp.exp(tops[n] - all_top) * ystat[n][:, 64:65]
-        scale = jnp.exp(plane_top - all_top) / grand
-
-    def y_copy(p, k):
-        return remote(
-            ybuf.at[p, y], ybuf.at[p, y], y_s.at[p, k - 1], y_r.at[p, k - 1], along_y(k)
-        )
-
-    def o_copy(p, k):
-        return remote(
-            obuf.at[p, y], obuf.at[p, y], o_s.at[p, k - 1], o_r.at[p, k - 1], along_y(k)
-        )
-
-    for p in range(PIPE):
-        with jax.named_scope("scwait"):
-            drain(recv.at[p, pl.ds(0, XZ - 1)], sc_r.at[p])
-        with jax.named_scope("reduce"):
-            mine = slice(p * PR, (p + 1) * PR)
-            acc = jnp.zeros((PR, D), F32)
-            for q in range(XZ):
-                acc = acc + flipped[mine, q : q + 1] * recv[p, q].astype(F32)
-            ybuf[p, y] = (acc * scale[mine]).astype(BF16)
-            for k in (2, 1, 3):
-                y_copy(p, k).start()
-
-    win_copy.wait()
-    wout_copy.wait()
-    per = PR // 4
-    expert = lax.broadcasted_iota(jnp.int32, (PR, H), 0) // 4
-    for p in range(PIPE):
-        with jax.named_scope("yex"):
-            for k in range(1, NY):
-                y_copy(p, k).wait()
-        with jax.named_scope("ffn"):
-            slot_in = jnp.sum(ybuf[p].astype(F32), axis=0).astype(BF16)
-            hidden = jnp.zeros((PR, H), F32)
-            for e in range(per):
-                hidden = jnp.where(expert == e, dot(slot_in, win[p * per + e]), hidden)
-            hidden = jax.nn.gelu(hidden).astype(BF16).astype(F32)
-            result = jnp.zeros((PR, D), F32)
-            for e in range(per):
-                result = result + dot(
-                    jnp.where(expert == e, hidden, 0.0).astype(BF16), wout[p * per + e]
-                )
-            obuf[p, y] = result
-            for k in (2, 1, 3):
-                o_copy(p, k).start()
+            grand = grand + scale[n] * ystat[n][:, 64:65]
+        scale = [v / grand for v in scale]
 
     def spread(p, k):
         block = so.at[p, xz, core]
@@ -287,12 +302,11 @@
         drain(so.at[p, pl.ds(0, n), 0], ag_r.at[p, dx])
         forward(p, dx).start()
 
-    for p in range(PIPE):
-        with jax.named_scope("oex"):
+    def publish(p):
+        with jax.named_scope(f"oex{p}"):
             for k in range(1, NY):
                 o_copy(p, k).wait()
-        with jax.named_scope("spread"):
-            so[p, xz, core] = (obuf[p, 0] + obuf[p, 1] + obuf[p, 2] + obuf[p, 3]).astype(BF16)
+            so[p, xz, core] = jnp.sum(obuf[p].astype(F32), axis=0).astype(BF16)
 
             def send_out(k, carry):
                 spread(p, k).start()
@@ -300,29 +314,52 @@
 
             lax.fori_loop(1, XZ, send_out, 0)
 
+    expert(0)
+    gather(3)
+    expert(1)
+    soft(5)
+    expert(2)
+    publish(0)
+    expert(3)
+    publish(1)
+    soft(6)
+    publish(2)
+    soft(7)
+    publish(3)
+
     def mix(i):
-        rows = pl.ds(pl.multiple_of(i * TCH, TCH), TCH)
-        mixed[rows, :] = dot(comb[rows, 0:SP], first[...])
-
+        rows = pl.ds(i * MCH, MCH)
+        mixed[rows, :] = dot(comb[rows, 0:SH], first[...])
+
+    turns = (0, 1, 3, 2)
     with jax.named_scope("agA"):
-        for dx in (0, 1, 3, 2):
-            arrive(0, dx)
-        for dx in range(NX):
-            forward(0, dx).wait()
-        first[...] = so[0].reshape(SP, D)
+        for p in range(PH):
+            for dx in turns:
+                arrive(p, dx)
+        for p in range(PH):
+            for dx in turns:
+                forward(p, dx).wait()
+        first[...] = so[0:PH].reshape(SH, D)
     with jax.named_scope("mixA"):
-        for i, dx in enumerate((0, 1, 3, 2)):
+        for i, dx in enumerate(turns):
             mix(i)
-            arrive(1, dx)
+            if i < 2:
+                arrive(2, turns[2 * i])
+                arrive(2, turns[2 * i + 1])
+            else:
+                arrive(3, turns[2 * i - 4])
+                arrive(3, turns[2 * i - 3])
     with jax.named_scope("agB"):
-        for dx in range(NX):
-            forward(1, dx).wait()
-        last[...] = so[1].reshape(SP, D)
-
-    drain(stats_recv.at[pl.ds(0, XZ - 1)], st_s)
-    for p in range(PIPE):
-        drain(recv.at[p, pl.ds(0, XZ - 1)], sc_s.at[p])
-        drain(recv.at[p, pl.ds(0, XZ - 1)], ag_s.at[p])
+        for p in range(PH, PIPE):
+            for dx in turns:
+                forward(p, dx).wait()
+        last[...] = so[PH:PIPE].reshape(SH, D)
+
+    with jax.named_scope("ends"):
+        drain(stats_recv.at[pl.ds(0, XZ - 1)], st_s)
+        for p in range(PIPE):
+            drain(recv.at[p, pl.ds(0, XZ - 1)], sc_s.at[p])
+            drain(recv.at[p, pl.ds(0, XZ - 1)], ag_s.at[p])
 
 
 def finish_kernel(mixed, comb, last, out, stage, sems):
@@ -332,7 +369,7 @@
 
     for i in range(TOK // SOFT):
         rows = pl.ds(i * SOFT, SOFT)
-        stage[rows, :] = (mixed[rows, :] + dot(comb[rows, SP:S], last[...])).astype(BF16)
+        stage[rows, :] = (mixed[rows, :] + dot(comb[rows, SH:S], last[...])).astype(BF16)
         out_copy(i).start()
     for i in range(TOK // SOFT):
         out_copy(i).wait()
@@ -346,7 +383,7 @@
     ]
     held = pl.pallas_call(
         layer_kernel,
-        out_shape=(vmem((TOK, D), F32), vmem((TOK, S), BF16), vmem((SP, D), BF16)),
+        out_shape=(vmem((TOK, D), F32), vmem((TOK, S), BF16), vmem((SH, D), BF16)),
         in_specs=[pl.BlockSpec(memory_space=pltpu.HBM)] * 4,
         out_specs=[pl.BlockSpec(memory_space=pltpu.VMEM)] * 3,
         scratch_shapes=[
@@ -355,11 +392,11 @@
             vmem((4, D, H), BF16),
             vmem((4, H, D), BF16),
             vmem((TOK, S), F32),
-            vmem((PIPE, SP, TOK), BF16),
+            vmem((2, SH, TOK), BF16),
             vmem((S, S), BF16),
-            vmem((PIPE, XZ, PR, D), F32),
-            vmem((PIPE, XZ, PR, D), BF16),
-            vmem((PIPE, XZ, PR, D), BF16),
+            vmem((2, XZ, HR, D), F32),
+            vmem((2, XZ, HR, D), BF16),
+            vmem((2, XZ, HR, D), BF16),
             vmem((PIPE, XZ, PR, D), BF16),
             vmem((PIPE, XZ, PR, D), BF16),
             vmem((8, S), F32),
@@ -368,13 +405,13 @@
             vmem((XZ, 1, 128), F32),
             vmem((NY, ROWS, 128), F32),
             vmem((PIPE, NY, PR, D), BF16),
-            vmem((PIPE, NY, PR, D), F32),
+            vmem((PIPE, NY, PR, D), BF16),
             vmem((PIPE, XZ, NC, PR, D), BF16),
-            vmem((SP, D), BF16),
+            vmem((SH, D), BF16),
             dma((NT + 1,)),
             dma((2,)),
             dma, dma,
-            dma((PIPE,)), dma((PIPE,)),
+            dma((2,)), dma((2,)),
             dma, dma,
             dma((PIPE,)), dma((PIPE,)),
             dma((NY - 1,)), dma((NY - 1,)),

time: 44.6 us -> 41.4 us (0.928)
  Pallas kernels: 44.4 us -> 41.3 us
    pallas_call x1, Pallas kernels: 42.1 us -> 38.9 us  [shards(): pl.pallas_call(layer_kernel, out_shape=(vmem((TOK, D), F32), vmem((TOK, S...]
where the time goes in v4:
time: 41.4 us; the launch traced here: 41.3 us
  Pallas kernels  41.3 us (100%)
    pallas_call x1, Pallas kernels, shards(): pl.pallas_call(layer_kernel, out_shape=(vmem((TOK, D), F32), vmem((TOK, S...  38.9 us
    pallas_call x1, Pallas kernels, shards(): pl.pallas_call(finish_kernel, out_shape=jax.ShapeDtypeStruct((TOK, D), BF...  2.38 us

profile of v4, /device:TPU:1, one launch (start us, length us, event | category | flops | bytes accessed | tf_op | source)
XLA Modules:
  0.0 41.3 jit_solution(436090879994440839)
XLA Ops:
  0.0 38.9 %layer.1 = (f32[2048,1024]{1,0:T(8,128)S(1)}, bf16[2048,512]{1,0:T(8,128)(2,1)S(1)}, bf16[256,1024]{1,0:T(8,128)(2,1)S(1)}) custom-call(bf16[2048,1024]{1,0:T(8,128)(2,1)} %tok_hbm.1, bf16[1024,512]{1,0:T(8,128)(2,1)} %par_hbm.1, bf16[4,1024,1024]{2,1,0:T(8,128)(2,1)} %win_hbm.1, bf16[4,1024,1024]{2,1,0:T(8,128)(2,1)} %wout_hbm.1), custom_call_target="tpu_custom_call" | custom-call | tf_op jit(solution)/shard_map/layer/pallas_call | solution.py:384
  38.9 2.4 %finish.1 = bf16[2048,1024]{1,0:T(8,128)(2,1)} custom-call(f32[2048,1024]{1,0:T(8,128)S(1)} %get-tuple-element.8.mixed, bf16[2048,512]{1,0:T(8,128)(2,1)S(1)} %get-tuple-element.9.comb, bf16[256,1024]{1,0:T(8,128)(2,1)S(1)} %get-tuple-element.10.last), custom_call_target="tpu_custom_call" | custom-call | tf_op jit(solution)/shard_map/finish/pallas_call | solution.py:428

commit v5 on v4

--- a/solution.py
+++ b/solution.py
@@ -20,6 +20,7 @@
 TCH = 512
 NT = TOK // TCH
 MCH = 512
+FAR_FIRST = (10, 9, 6, 11, 14, 5, 7, 13, 15, 8, 2, 4, 1, 12, 3)
 SOFT = 256
 
 
@@ -74,14 +75,11 @@
     def greet(to):
         pl.semaphore_signal(barrier, inc=1, device_id=to, device_id_type=MESH)
 
-    def greet_plane(k, carry):
-        greet(device(where_is(k)))
-        return carry
-
     greet(other)
     for k in range(1, NY):
         greet(along_y(k))
-    lax.fori_loop(1, XZ, greet_plane, 0)
+    for k in range(1, XZ):
+        greet(device(where_is(k)))
     for i in range(1, NT):
         tok_copy(i).start()
 
@@ -160,14 +158,11 @@
         turned = turned.reshape(XZ, NC, ROWS, 128)
         factors = jnp.where(core == 0, turned[:, 0], turned[:, 1])
 
-        def send_stats(k, carry):
+        for k in FAR_FIRST:
             to_xz = where_is(k)
             remote(
                 stats.at[to_xz * NC + core], stats_recv.at[xz], st_s, st_r, device(to_xz)
             ).start()
-            return carry
-
-        lax.fori_loop(1, XZ, send_stats, 0)
         stats_recv[xz] = stats[wide]
 
     def send_step(h):
@@ -177,15 +172,11 @@
         for p in range(h * PH, (h + 1) * PH):
             outb[p] = joined[:, (p % PH) * PR : (p % PH + 1) * PR]
         for p in range(h * PH, (h + 1) * PH):
-
-            def send(k, carry):
+            for k in FAR_FIRST:
                 to_xz = where_is(k)
                 remote(
-                    outb.at[p, to_xz], recv.at[p, xz], sc_s.at[p], sc_r.at[p], device(to_xz)
+                    outb.at[p, to_xz], recv.at[p, xz], sc_s, sc_r.at[p], device(to_xz)
                 ).start()
-                return carry
-
-            lax.fori_loop(1, XZ, send, 0)
             recv[p, xz] = outb[p, xz]
 
     def soften(i, carry):
@@ -198,17 +189,16 @@
 
     with jax.named_scope("send0"):
         send_step(0)
-    with jax.named_scope("soft0"):
+    with jax.named_scope("send1"):
+        send_step(1)
+    with jax.named_scope("order"):
         new = lax.broadcasted_iota(jnp.int32, (S, S), 1)
         old = lax.broadcasted_iota(jnp.int32, (S, S), 0)
         within = new % SP
         source = (within // PR) * ROWS + (new // SP) * PR + within % PR
         order[...] = jnp.where(old == source, 1.0, 0.0).astype(BF16)
-        lax.fori_loop(0, 1, soften, 0)
-    with jax.named_scope("send1"):
-        send_step(1)
     with jax.named_scope("soft1"):
-        lax.fori_loop(1, 3, soften, 0)
+        lax.fori_loop(0, 3, soften, 0)
 
     with jax.named_scope("ystat"):
         drain(stats_recv.at[pl.ds(0, XZ - 1)], st_r)
@@ -225,7 +215,7 @@
         ystat[y] = jnp.where(lane2 < 64, plane_top, plane_total)
 
         def ystat_copy(k):
-            return remote(ystat.at[y], ystat.at[y], yst_s.at[k - 1], yst_r.at[k - 1], along_y(k))
+            return remote(ystat.at[y], ystat.at[y], yst_s, yst_r, along_y(k))
 
         for k in (2, 1, 3):
             ystat_copy(k).start()
@@ -235,12 +225,12 @@
 
     def y_copy(p, k):
         return remote(
-            ybuf.at[p, y], ybuf.at[p, y], y_s.at[p, k - 1], y_r.at[p, k - 1], along_y(k)
+            ybuf.at[p, y], ybuf.at[p, y], y_s, y_r.at[p], along_y(k)
         )
 
     def o_copy(p, k):
         return remote(
-            obuf.at[p, y], obuf.at[p, y], o_s.at[p, k - 1], o_r.at[p, k - 1], along_y(k)
+            obuf.at[p, y], obuf.at[p, y], o_s, o_r.at[p], along_y(k)
         )
 
     def gather(p):
@@ -256,8 +246,7 @@
 
     def expert(p):
         with jax.named_scope(f"ffn{p}"):
-            for k in range(1, NY):
-                y_copy(p, k).wait()
+            drain(recv.at[p, pl.ds(0, 3)], y_r.at[p])
             mine = slice(p * PR, (p + 1) * PR)
             acc = jnp.zeros((PR, D), F32)
             for n in range(NY):
@@ -278,8 +267,7 @@
     with jax.named_scope("ystatw"):
         win_copy.wait()
         wout_copy.wait()
-        for k in range(1, NY):
-            ystat_copy(k).wait()
+        drain(ystat.at[pl.ds(0, 3)], yst_r)
         tops = [ystat[n][:, 0:1] for n in range(NY)]
         all_top = jnp.maximum(jnp.maximum(tops[0], tops[1]), jnp.maximum(tops[2], tops[3]))
         scale = [jnp.exp(tops[n] - all_top) for n in range(NY)]
@@ -290,12 +278,12 @@
 
     def spread(p, k):
         block = so.at[p, xz, core]
-        return remote(block, block, ag_s.at[p], ag_r.at[p, k // NZ], device(where_is(k)))
+        return remote(block, block, ag_s, ag_r.at[p, k // NZ], device(where_is(k)))
 
     def forward(p, dx):
         fx = (x - dx + NX) % NX
         block = so.at[p, pl.ds(fx * NZ, NZ), core]
-        return remote(block, block, fw_s.at[p, dx], fw_r.at[p, dx], other)
+        return remote(block, block, fw_s, fw_r.at[p // PH], other)
 
     def arrive(p, dx):
         n = NZ - (1 if dx == 0 else 0)
@@ -304,15 +292,10 @@
 
     def publish(p):
         with jax.named_scope(f"oex{p}"):
-            for k in range(1, NY):
-                o_copy(p, k).wait()
+            drain(recv.at[p, pl.ds(0, 3)], o_r.at[p])
             so[p, xz, core] = jnp.sum(obuf[p].astype(F32), axis=0).astype(BF16)
-
-            def send_out(k, carry):
+            for k in FAR_FIRST:
                 spread(p, k).start()
-                return carry
-
-            lax.fori_loop(1, XZ, send_out, 0)
 
     expert(0)
     gather(3)
@@ -336,9 +319,7 @@
         for p in range(PH):
             for dx in turns:
                 arrive(p, dx)
-        for p in range(PH):
-            for dx in turns:
-                forward(p, dx).wait()
+        drain(recv.at[pl.ds(0, PH)], fw_r.at[0])
         first[...] = so[0:PH].reshape(SH, D)
     with jax.named_scope("mixA"):
         for i, dx in enumerate(turns):
@@ -350,16 +331,17 @@
                 arrive(3, turns[2 * i - 4])
                 arrive(3, turns[2 * i - 3])
     with jax.named_scope("agB"):
-        for p in range(PH, PIPE):
-            for dx in turns:
-                forward(p, dx).wait()
+        drain(recv.at[pl.ds(0, PH)], fw_r.at[1])
         last[...] = so[PH:PIPE].reshape(SH, D)
 
     with jax.named_scope("ends"):
         drain(stats_recv.at[pl.ds(0, XZ - 1)], st_s)
-        for p in range(PIPE):
-            drain(recv.at[p, pl.ds(0, XZ - 1)], sc_s.at[p])
-            drain(recv.at[p, pl.ds(0, XZ - 1)], ag_s.at[p])
+        drain(recv.at[:, pl.ds(0, XZ - 1)], sc_s)
+        drain(ystat.at[pl.ds(0, 3)], yst_s)
+        drain(recv.at[:, pl.ds(0, 3)], y_s)
+        drain(recv.at[:, pl.ds(0, 3)], o_s)
+        drain(recv.at[:, pl.ds(0, XZ - 1)], ag_s)
+        drain(recv, fw_s)
 
 
 def finish_kernel(mixed, comb, last, out, stage, sems):
@@ -413,12 +395,12 @@
             dma, dma,
             dma((2,)), dma((2,)),
             dma, dma,
-            dma((PIPE,)), dma((PIPE,)),
-            dma((NY - 1,)), dma((NY - 1,)),
-            dma((PIPE, NY - 1)), dma((PIPE, NY - 1)),
-            dma((PIPE, NY - 1)), dma((PIPE, NY - 1)),
-            dma((PIPE,)), dma((PIPE, NX)),
-            dma((PIPE, NX)), dma((PIPE, NX)),
+            dma, dma((PIPE,)),
+            dma, dma,
+            dma, dma((PIPE,)),
+            dma, dma((PIPE,)),
+            dma, dma((PIPE, NX)),
+            dma, dma((2,)),
         ],
         compiler_params=pltpu.CompilerParams(
             collective_id=0, has_side_effects=True, vmem_limit_bytes=48 * 1024 * 1024

time: 41.4 us -> 39.3 us (0.949)
  Pallas kernels: 41.3 us -> 39.2 us
    pallas_call x1, Pallas kernels: 38.9 us -> 36.8 us  [shards(): pl.pallas_call(layer_kernel, out_shape=(vmem((TOK, D), F32), vmem((TOK, S...]
where the time goes in v5:
time: 39.3 us; the launch traced here: 39.2 us
  Pallas kernels  39.2 us (100%)
    pallas_call x1, Pallas kernels, shards(): pl.pallas_call(layer_kernel, out_shape=(vmem((TOK, D), F32), vmem((TOK, S...  36.8 us
    pallas_call x1, Pallas kernels, shards(): pl.pallas_call(finish_kernel, out_shape=jax.ShapeDtypeStruct((TOK, D), BF...  2.38 us

profile of v5, /device:TPU:1, one launch (start us, length us, event | category | flops | bytes accessed | tf_op | source)
XLA Modules:
  0.0 39.2 jit_solution(17556850158169380354)
XLA Ops:
  0.0 36.8 %layer.1 = (f32[2048,1024]{1,0:T(8,128)S(1)}, bf16[2048,512]{1,0:T(8,128)(2,1)S(1)}, bf16[256,1024]{1,0:T(8,128)(2,1)S(1)}) custom-call(bf16[2048,1024]{1,0:T(8,128)(2,1)} %tok_hbm.1, bf16[1024,512]{1,0:T(8,128)(2,1)} %par_hbm.1, bf16[4,1024,1024]{2,1,0:T(8,128)(2,1)} %win_hbm.1, bf16[4,1024,1024]{2,1,0:T(8,128)(2,1)} %wout_hbm.1), custom_call_target="tpu_custom_call" | custom-call | tf_op jit(solution)/shard_map/layer/pallas_call | solution.py:366
  36.8 2.4 %finish.1 = bf16[2048,1024]{1,0:T(8,128)(2,1)} custom-call(f32[2048,1024]{1,0:T(8,128)S(1)} %get-tuple-element.8.mixed, bf16[2048,512]{1,0:T(8,128)(2,1)S(1)} %get-tuple-element.9.comb, bf16[256,1024]{1,0:T(8,128)(2,1)S(1)} %get-tuple-element.10.last), custom_call_target="tpu_custom_call" | custom-call | tf_op jit(solution)/shard_map/finish/pallas_call | solution.py:410

commit v6 on v5

--- a/solution.py
+++ b/solution.py
@@ -67,8 +67,11 @@
         return pltpu.make_async_copy(tok_hbm.at[rows], tok.at[rows], in_sem.at[i])
 
     par_copy = pltpu.make_async_copy(par_hbm, par, in_sem.at[NT])
-    par_copy.start()
-    tok_copy(0).start()
+    for i in range(4):
+        rows = pl.ds(i * (D // 4), D // 4)
+        pltpu.make_async_copy(par_hbm.at[rows], par.at[rows], in_sem.at[NT]).start()
+        rows = pl.ds(i * (TCH // 4), TCH // 4)
+        pltpu.make_async_copy(tok_hbm.at[rows], tok.at[rows], in_sem.at[0]).start()
 
     barrier = pltpu.get_barrier_semaphore()
 
@@ -130,7 +133,7 @@
     def share_block(h, block):
         block = block.reshape(XZ, NC, HR, D)
         own[h] = jnp.where(core == 0, block[:, 0], block[:, 1])
-        give[h] = jnp.where(core == 0, block[:, 1], block[:, 0]).astype(BF16)
+        give[h] = jnp.where(core == 0, block[:, 1], block[:, 0])
         part_copy(h).start()
 
     with jax.named_scope("mm0"):
@@ -168,7 +171,7 @@
     def send_step(h):
         part_copy(h).wait()
         f = factors[:, h * HR : (h + 1) * HR]
-        joined = (f[:, :, 0:1] * own[h] + f[:, :, 32:33] * part[h].astype(F32)).astype(BF16)
+        joined = (f[:, :, 0:1] * own[h] + f[:, :, 32:33] * part[h]).astype(BF16)
         for p in range(h * PH, (h + 1) * PH):
             outb[p] = joined[:, (p % PH) * PR : (p % PH + 1) * PR]
         for p in range(h * PH, (h + 1) * PH):
@@ -278,16 +281,20 @@
 
     def spread(p, k):
         block = so.at[p, xz, core]
-        return remote(block, block, ag_s, ag_r.at[p, k // NZ], device(where_is(k)))
+        return remote(block, block, ag_s, ag_r.at[p if p < PIPE - 1 else p + k // NZ], device(where_is(k)))
 
     def forward(p, dx):
         fx = (x - dx + NX) % NX
         block = so.at[p, pl.ds(fx * NZ, NZ), core]
         return remote(block, block, fw_s, fw_r.at[p // PH], other)
 
-    def arrive(p, dx):
-        n = NZ - (1 if dx == 0 else 0)
-        drain(so.at[p, pl.ds(0, n), 0], ag_r.at[p, dx])
+    def arrive(p):
+        drain(recv.at[p, pl.ds(0, XZ - 1)], ag_r.at[p])
+        block = so.at[p, :, core]
+        remote(block, block, fw_s, fw_r.at[p // PH], other).start()
+
+    def arrive_row(p, dx):
+        drain(so.at[p, pl.ds(0, NZ - (1 if dx == 0 else 0)), 0], ag_r.at[p + dx])
         forward(p, dx).start()
 
     def publish(p):
@@ -317,19 +324,17 @@
     turns = (0, 1, 3, 2)
     with jax.named_scope("agA"):
         for p in range(PH):
-            for dx in turns:
-                arrive(p, dx)
+            arrive(p)
         drain(recv.at[pl.ds(0, PH)], fw_r.at[0])
         first[...] = so[0:PH].reshape(SH, D)
     with jax.named_scope("mixA"):
-        for i, dx in enumerate(turns):
-            mix(i)
-            if i < 2:
-                arrive(2, turns[2 * i])
-                arrive(2, turns[2 * i + 1])
-            else:
-                arrive(3, turns[2 * i - 4])
-                arrive(3, turns[2 * i - 3])
+        mix(0)
+        mix(1)
+        arrive(2)
+        mix(2)
+        for dx in turns:
+            arrive_row(3, dx)
+        mix(3)
     with jax.named_scope("agB"):
         drain(recv.at[pl.ds(0, PH)], fw_r.at[1])
         last[...] = so[PH:PIPE].reshape(SH, D)
@@ -377,8 +382,8 @@
             vmem((2, SH, TOK), BF16),
             vmem((S, S), BF16),
             vmem((2, XZ, HR, D), F32),
-            vmem((2, XZ, HR, D), BF16),
-            vmem((2, XZ, HR, D), BF16),
+            vmem((2, XZ, HR, D), F32),
+            vmem((2, XZ, HR, D), F32),
             vmem((PIPE, XZ, PR, D), BF16),
             vmem((PIPE, XZ, PR, D), BF16),
             vmem((8, S), F32),
@@ -399,7 +404,7 @@
             dma, dma,
             dma, dma((PIPE,)),
             dma, dma((PIPE,)),
-            dma, dma((PIPE, NX)),
+            dma, dma((PIPE - 1 + NX,)),
             dma, dma((2,)),
         ],
         compiler_params=pltpu.CompilerParams(

time: 39.3 us -> 39 us (level)
  no operation moved by 1% of the time
where the time goes in v6:
time: 39 us; the launch traced here: 38.9 us
  Pallas kernels  38.9 us (100%)
    pallas_call x1, Pallas kernels, shards(): pl.pallas_call(layer_kernel, out_shape=(vmem((TOK, D), F32), vmem((TOK, S...  36.5 us
    pallas_call x1, Pallas kernels, shards(): pl.pallas_call(finish_kernel, out_shape=jax.ShapeDtypeStruct((TOK, D), BF...  2.38 us

profile of v6, /device:TPU:1, one launch (start us, length us, event | category | flops | bytes accessed | tf_op | source)
XLA Modules:
  0.0 38.9 jit_solution(12597847974641887861)
XLA Ops:
  0.0 36.5 %layer.1 = (f32[2048,1024]{1,0:T(8,128)S(1)}, bf16[2048,512]{1,0:T(8,128)(2,1)S(1)}, bf16[256,1024]{1,0:T(8,128)(2,1)S(1)}) custom-call(bf16[2048,1024]{1,0:T(8,128)(2,1)} %tok_hbm.1, bf16[1024,512]{1,0:T(8,128)(2,1)} %par_hbm.1, bf16[4,1024,1024]{2,1,0:T(8,128)(2,1)} %win_hbm.1, bf16[4,1024,1024]{2,1,0:T(8,128)(2,1)} %wout_hbm.1), custom_call_target="tpu_custom_call" | custom-call | tf_op jit(solution)/shard_map/layer/pallas_call | solution.py:371
  36.5 2.4 %finish.1 = bf16[2048,1024]{1,0:T(8,128)(2,1)} custom-call(f32[2048,1024]{1,0:T(8,128)S(1)} %get-tuple-element.8.mixed, bf16[2048,512]{1,0:T(8,128)(2,1)S(1)} %get-tuple-element.9.comb, bf16[256,1024]{1,0:T(8,128)(2,1)S(1)} %get-tuple-element.10.last), custom_call_target="tpu_custom_call" | custom-call | tf_op jit(solution)/shard_map/finish/pallas_call | solution.py:415

commit v7 on v6

--- a/solution.py
+++ b/solution.py
@@ -133,14 +133,20 @@
     def share_block(h, block):
         block = block.reshape(XZ, NC, HR, D)
         own[h] = jnp.where(core == 0, block[:, 0], block[:, 1])
-        give[h] = jnp.where(core == 0, block[:, 1], block[:, 0])
+        give[h] = jnp.where(core == 0, block[:, 1], block[:, 0]).astype(BF16)
         part_copy(h).start()
 
     with jax.named_scope("mm0"):
         share_block(0, block)
 
+    def stash(lo):
+        cols = slice(lo, lo + D // 2)
+        block = dot(disp_t[1], tok[:, cols]).reshape(XZ, NC, HR, D // 2)
+        own[1, :, :, cols] = jnp.where(core == 0, block[:, 0], block[:, 1])
+        give[1, :, :, cols] = jnp.where(core == 0, block[:, 1], block[:, 0]).astype(BF16)
+
     with jax.named_scope("mm1"):
-        share_block(1, dot(disp_t[1], tok[...]))
+        stash(0)
 
     with jax.named_scope("stats"):
         core_copy.wait()
@@ -171,7 +177,7 @@
     def send_step(h):
         part_copy(h).wait()
         f = factors[:, h * HR : (h + 1) * HR]
-        joined = (f[:, :, 0:1] * own[h] + f[:, :, 32:33] * part[h]).astype(BF16)
+        joined = (f[:, :, 0:1] * own[h] + f[:, :, 32:33] * part[h].astype(F32)).astype(BF16)
         for p in range(h * PH, (h + 1) * PH):
             outb[p] = joined[:, (p % PH) * PR : (p % PH + 1) * PR]
         for p in range(h * PH, (h + 1) * PH):
@@ -192,8 +198,9 @@
 
     with jax.named_scope("send0"):
         send_step(0)
-    with jax.named_scope("send1"):
-        send_step(1)
+    with jax.named_scope("mm2"):
+        stash(D // 2)
+        part_copy(1).start()
     with jax.named_scope("order"):
         new = lax.broadcasted_iota(jnp.int32, (S, S), 1)
         old = lax.broadcasted_iota(jnp.int32, (S, S), 0)
@@ -201,7 +208,11 @@
         source = (within // PR) * ROWS + (new // SP) * PR + within % PR
         order[...] = jnp.where(old == source, 1.0, 0.0).astype(BF16)
     with jax.named_scope("soft1"):
-        lax.fori_loop(0, 3, soften, 0)
+        lax.fori_loop(0, 1, soften, 0)
+    with jax.named_scope("send1"):
+        send_step(1)
+    with jax.named_scope("soft1b"):
+        lax.fori_loop(1, 3, soften, 0)
 
     with jax.named_scope("ystat"):
         drain(stats_recv.at[pl.ds(0, XZ - 1)], st_r)
@@ -382,8 +393,8 @@
             vmem((2, SH, TOK), BF16),
             vmem((S, S), BF16),
             vmem((2, XZ, HR, D), F32),
-            vmem((2, XZ, HR, D), F32),
-            vmem((2, XZ, HR, D), F32),
+            vmem((2, XZ, HR, D), BF16),
+            vmem((2, XZ, HR, D), BF16),
             vmem((PIPE, XZ, PR, D), BF16),
             vmem((PIPE, XZ, PR, D), BF16),
             vmem((8, S), F32),

time: 39 us -> 38.6 us (0.990)
  Pallas kernels: 38.9 us -> 38.5 us
    pallas_call x1, Pallas kernels: 36.5 us -> 36.1 us  [shards(): pl.pallas_call(layer_kernel, out_shape=(vmem((TOK, D), F32), vmem((TOK, S...]
where the time goes in v7:
time: 38.6 us; the launch traced here: 38.5 us
  Pallas kernels  38.5 us (100%)
    pallas_call x1, Pallas kernels, shards(): pl.pallas_call(layer_kernel, out_shape=(vmem((TOK, D), F32), vmem((TOK, S...  36.1 us
    pallas_call x1, Pallas kernels, shards(): pl.pallas_call(finish_kernel, out_shape=jax.ShapeDtypeStruct((TOK, D), BF...  2.38 us

profile of v7, /device:TPU:1, one launch (start us, length us, event | category | flops | bytes accessed | tf_op | source)
XLA Modules:
  0.0 38.5 jit_solution(8658029507605863713)
XLA Ops:
  0.0 36.1 %layer.1 = (f32[2048,1024]{1,0:T(8,128)S(1)}, bf16[2048,512]{1,0:T(8,128)(2,1)S(1)}, bf16[256,1024]{1,0:T(8,128)(2,1)S(1)}) custom-call(bf16[2048,1024]{1,0:T(8,128)(2,1)} %tok_hbm.1, bf16[1024,512]{1,0:T(8,128)(2,1)} %par_hbm.1, bf16[4,1024,1024]{2,1,0:T(8,128)(2,1)} %win_hbm.1, bf16[4,1024,1024]{2,1,0:T(8,128)(2,1)} %wout_hbm.1), custom_call_target="tpu_custom_call" | custom-call | tf_op jit(solution)/shard_map/layer/pallas_call | solution.py:382
  36.1 2.4 %finish.1 = bf16[2048,1024]{1,0:T(8,128)(2,1)} custom-call(f32[2048,1024]{1,0:T(8,128)S(1)} %get-tuple-element.8.mixed, bf16[2048,512]{1,0:T(8,128)(2,1)S(1)} %get-tuple-element.9.comb, bf16[256,1024]{1,0:T(8,128)(2,1)S(1)} %get-tuple-element.10.last), custom_call_target="tpu_custom_call" | custom-call | tf_op jit(solution)/shard_map/finish/pallas_call | solution.py:426
